TPU v7x, 32 devices: a whole 2x2x4 slice. The times are simulated.
32 devices in a mesh: gx: 4 (over y, x), gy: 8 (over z, core).
Axes of the slice: x: 2, y: 2, z: 4, core: 2. Of those that a mesh axis runs over, the one named last changes fastest.
Arguments:
- inputs: bfloat16 [512, 8192], P('gx', 'gy'), may hold values from -6 to 6
- out_grad: bfloat16 [512, 8192], P('gx', 'gy'), may hold values from -1.1953125 to 1.1953125
- pre_act: bfloat16 [512, 32768], P('gy', 'gx'), may hold values from -6 to 6
- w_in: bfloat16 [8192, 32768], P('gy', 'gx'), may hold values from -0.0625 to 0.0625
- w_out: bfloat16 [32768, 8192], P('gx', 'gy'), may hold values from -0.03125 to 0.03125
- counts: int32 [4], replicated, may hold values from 1 to 128, 320 in all
Outputs:
- in_grad: bfloat16 [512, 8192], P('gx', 'gy')
- w_in_grad: bfloat16 [8192, 32768], P('gy', 'gx')
- w_out_grad: bfloat16 [32768, 8192], P('gx', 'gy')
Inputs may be any that keep to these rules, and one draw needn't show every extreme that they name: In batch shard s (token slots s * 128 to (s + 1) * 128 - 1) the first counts[s] slots are live and the rest are padding; the counts add up to exactly 320, and at least one shard is full.
All inputs are finite; a program needn't handle non-finite values.
Results may differ from a plain program's by a relative error of at most 0.0051.
Values may be sent and summed in bfloat16 or wider, within the bound.
No kernel may reach another device: no remote copies, remote signals or barrier semaphores. Data moves between devices by JAX's collectives and lax.ppermute only.
A program may use at most 192 MiB of HBM per device.

v0:
```python
import math

import jax
import jax.numpy as jnp
from jax import lax
from jax.sharding import PartitionSpec as P

gelu_scale = math.sqrt(2.0 / math.pi)
cubic_coef = 0.044715


def gelu_value(pre):
    tangent = jnp.tanh(gelu_scale * (pre + cubic_coef * pre * pre * pre))
    return 0.5 * pre * (1.0 + tangent)


def gelu_slope(pre):
    tangent = jnp.tanh(gelu_scale * (pre + cubic_coef * pre * pre * pre))
    return 0.5 * (1.0 + tangent) + 0.5 * pre * (1.0 - tangent * tangent) * gelu_scale * (
        1.0 + 3.0 * cubic_coef * pre * pre
    )


def token_sum(left, right):
    return lax.dot_general(
        left, right, (((0,), (0,)), ((), ())), preferred_element_type=jnp.float32
    )


def contract_last(left, right):
    return lax.dot_general(
        left, right, (((1,), (1,)), ((), ())), preferred_element_type=jnp.float32
    )


def live_mask(counts, shard_rows, all_rows, shards):
    positions = jnp.arange(all_rows, dtype=jnp.int32)
    owner_shard = positions // shard_rows
    one_hot = owner_shard[:, None] == jnp.arange(shards, dtype=jnp.int32)[None, :]
    own_count = jnp.sum(jnp.where(one_hot, counts[None, :], 0), axis=1)
    return positions % shard_rows < own_count


def packed_index(counts, shard_rows, shards, live_rows):
    ends = jnp.cumsum(counts)
    starts = ends - counts
    packed = jnp.arange(live_rows, dtype=jnp.int32)
    which = jnp.sum((ends[None, :] <= packed[:, None]).astype(jnp.int32), axis=1)
    one_hot = which[:, None] == jnp.arange(shards, dtype=jnp.int32)[None, :]
    begin = jnp.sum(jnp.where(one_hot, starts[None, :], 0), axis=1)
    return which * shard_rows + packed - begin


def body(inputs, out_grad, pre_act, w_in, w_out, counts):
    shard_rows = inputs.shape[0]
    shards = lax.axis_size("gx")
    all_rows = shard_rows * shards
    live_rows = all_rows * 5 // 8
    row_index = packed_index(counts, shard_rows, shards, live_rows)
    gathered_x, gathered_dy = (
        lax.all_gather(inputs, "gx", axis=0, tiled=True),
        lax.all_gather(out_grad, "gx", axis=0, tiled=True),
    )
    is_live = live_mask(counts, shard_rows, all_rows, shards)
    masked_grad = jnp.where(is_live[:, None], gathered_dy, jnp.zeros_like(gathered_dy))
    whole_pre = lax.all_gather(pre_act, "gy", axis=0, tiled=True).astype(jnp.float32)
    activation = gelu_value(whole_pre).astype(jnp.bfloat16)
    sent_grad = jnp.take(masked_grad, row_index, axis=0)
    sent_pre = jnp.take(whole_pre, row_index, axis=0)
    hidden_total = lax.psum(contract_last(sent_grad, w_out), "gy")
    sent_hidden = (hidden_total * gelu_slope(sent_pre)).astype(jnp.bfloat16)
    hidden_grad = (
        jnp.zeros((all_rows, sent_hidden.shape[1]), jnp.bfloat16).at[row_index].set(sent_hidden)
    )
    w_out_grad = token_sum(activation, masked_grad)
    w_in_grad = token_sum(gathered_x, hidden_grad)
    in_part = lax.psum_scatter(
        contract_last(hidden_grad, w_in), "gx", scatter_dimension=0, tiled=True
    )
    return (
        in_part.astype(jnp.bfloat16),
        w_in_grad.astype(jnp.bfloat16),
        w_out_grad.astype(jnp.bfloat16),
    )


def solution(mesh):
    return jax.shard_map(
        body,
        mesh=mesh,
        in_specs=(P("gx", "gy"), P("gx", "gy"), P("gy", "gx"), P("gy", "gx"), P("gx", "gy"), P()),
        out_specs=(P("gx", "gy"), P("gy", "gx"), P("gx", "gy")),
        check_vma=False,
    )
```

profile of v0, /device:TPU:0, one launch (start us, length us, event | category | flops | bytes accessed | tf_op | source)
XLA Modules:
  0.0 445.7 jit_solution(4498768962344689414)
XLA Ops:
  7.2 0.7 all-gather.4.cloned.1.call-update
  7.9 0.7 all-gather.6.cloned.1.call-update
  8.7 0.8 reduce-window.8
  9.5 0.1 convert_reduce_fusion
  9.6 0.7 bitcast_subtract_fusion
  10.3 0.1 select_reduce_fusion.1
  10.4 0.7 select_reduce_fusion
  11.2 27.9 %all-gather.4.cloned.1.call-done = bf16[512,1024]{1,0:T(8,128)(2,1)} async-done(((bf16[128,1024]{1,0:T(8,128)(2,1)}), bf16[512,1024]{1,0:T(8,128)(2,1)}) %all-gather.4.cloned.1.call-update) | async-done | bytes 1048592 | tf_op jit(solution)/shard_map/all_gather | solution.py:62
  39.1 1.4 broadcast_select_fusion
  40.5 2.1 gather_fusion
  42.6 19.9 %fusion.20 = f32[320,8192]{1,0:T(8,128)} fusion(bf16[8192,1024]{1,0:T(8,128)(2,1)} %param.10, bf16[320,1024]{1,0:T(8,128)(2,1)S(1)} %gather_fusion, pred[320]{0:T(512)(128)(4,1)S(1)} %compare_and_fusion), kind=kOutput, calls=%fused_computation.28 | convolution fusion | flops 5369036800 | bytes 27918656 | tf_op jit(solution)/shard_map/dot_general | solution.py:31
  62.6 0.5 all-gather.8.cloned.1.call-update
  63.1 0.6 reduce-scatter.2.cloned.1.call-start
  63.7 59.1 %all-gather.6.cloned.1.call-done = bf16[512,8192]{1,0:T(8,128)(2,1)} async-done(((bf16[64,8192]{1,0:T(8,128)(2,1)}), bf16[512,8192]{1,0:T(8,128)(2,1)}) %all-gather.6.cloned.1.call-update) | async-done | bytes 8388624 | tf_op jit(solution)/shard_map/all_gather | solution.py:66
  122.8 12.1 %convert_element_type.25 = f32[512,8192]{1,0:T(8,128)} convert(bf16[512,8192]{1,0:T(8,128)(2,1)} %all-gather.6.cloned.1.call-done) | non-fusion elementwise | flops 4194304 | bytes 25165824 | tf_op jit(solution)/shard_map/convert_element_type | solution.py:66
  134.9 19.9 %gather_fusion.1 = f32[320,8192]{1,0:T(8,128)} fusion(f32[512,8192]{1,0:T(8,128)} %convert_element_type.25, s32[1024]{0:T(1024)S(1)} %pad_clamp_fusion), kind=kCustom, calls=%fused_computation.1 | custom fusion | bytes 20972800 | tf_op jit(solution)/shard_map/jit(_take)/gather | solution.py:69
  154.8 184.5 %all-reduce.2.cloned.1.call-done = f32[320,8192]{1,0:T(8,128)} async-done(((f32[320,8192]{1,0:T(8,128)}), f32[320,8192]{1,0:T(8,128)}) %all-reduce.2.cloned.1.call-update) | async-done | bytes 10485776 | tf_op jit(solution)/shard_map/psum | solution.py:70
  339.3 12.5 %fusion.11 = bf16[320,8192]{1,0:T(8,128)(2,1)} fusion(f32[320,8192]{1,0:T(8,128)} %all-reduce.2.cloned.1.call-done, f32[320,8192]{1,0:T(8,128)} %gather_fusion.1, pred[320]{0:T(512)(128)(4,1)S(1)} %compare_and_fusion), kind=kLoop, calls=%fused_computation.19 | loop fusion | flops 52428800 | bytes 26214720 | tf_op jit(solution)/shard_map/convert_element_type | solution.py:71
  351.8 14.2 %scatter_custom_fusion = bf16[512,8192]{1,0:T(8,128)(2,1)} fusion(s32[320]{0:T(512)S(1)} %fusion.30, bf16[320,8192]{1,0:T(8,128)(2,1)} %fusion.11, bf16[]{:T(256)} %constant.45.clone.1), kind=kCustom, calls=%fused_computation.25 | custom fusion | bytes 8389120 | tf_op jit(solution)/shard_map/scatter | solution.py:73
  366.0 16.0 %fusion.36 = f32[512,1024]{1,0:T(8,128)} fusion(bf16[512,8192]{1,0:T(8,128)(2,1)} %scatter_custom_fusion, bf16[1024,8192]{1,0:T(8,128)(2,1)} %param.9), kind=kOutput, calls=%fused_computation.61 | convolution fusion | flops 8589934592 | bytes 27262976 | tf_op jit(solution)/shard_map/dot_general | solution.py:31
  382.0 15.1 %convert_bitcast_fusion = bf16[1024,8192]{0,1:T(8,128)(2,1)} fusion(bf16[512,8192]{1,0:T(8,128)(2,1)} %scatter_custom_fusion, bf16[512,1024]{1,0:T(8,128)(2,1)} %all-gather.8.cloned.1.call-done), kind=kOutput, calls=%fused_computation.9 | convolution fusion | flops 8598323200 | bytes 26214400 | tf_op jit(solution)/shard_map/dot_general | solution.py:25
  397.1 21.3 %copy.11 = bf16[1024,8192]{1,0:T(8,128)(2,1)} copy(bf16[1024,8192]{0,1:T(8,128)(2,1)} %convert_bitcast_fusion) | data formatting | bytes 33554432
  418.4 18.7 %convolution_convert_fusion = bf16[8192,1024]{1,0:T(8,128)(2,1)} fusion(bf16[512,1024]{1,0:T(8,128)(2,1)S(1)} %broadcast_select_fusion, bf16[512,8192]{1,0:T(8,128)(2,1)} %all-gather.6.cloned.1.call-done), kind=kOutput, calls=%fused_computation.12 | convolution fusion | flops 8640266240 | bytes 26214400 | tf_op jit(solution)/shard_map/dot_general | solution.py:25
  437.1 1.8 convert_element_type.27
  (14 shorter events, 0.3 us)
Async XLA Ops:
  7.2 31.9 %all-gather.4.cloned.1.call-start = ((), (), s32[]{:S(2)}) async-start(), calls=%async_computation.1 | async-start | bytes 1310720 | tf_op jit(solution)/shard_map/all_gather | solution.py:62
  7.9 114.9 %all-gather.6.cloned.1.call-start = ((), (), s32[]{:S(2)}) async-start(), calls=%async_computation.3 | async-start | bytes 9437184 | tf_op jit(solution)/shard_map/all_gather | solution.py:66
  8.6 330.6 %all-reduce.2.cloned.1.call-start = ((), (), s32[]{:S(2)}) async-start(), calls=%async_computation.2 | async-start | bytes 20971520 | tf_op jit(solution)/shard_map/psum | solution.py:70
  62.5 319.5 %all-gather.8.cloned.1.call-start = ((), (), s32[]{:S(2)}) async-start(), calls=%async_computation.5 | async-start | bytes 1310720 | tf_op jit(solution)/shard_map/all_gather | solution.py:61
  63.1 374.0 %reduce-scatter.2.cloned.1.call-start = ((), (), s32[]{:S(2)}) async-start(), calls=%async_computation.4 | async-start | bytes 2621440 | tf_op jit(solution)/shard_map/reduce_scatter | solution.py:77
Sparse Core Ops, SparseCore 0:
  9.8 29.2 all-gather.3
  40.7 82.0 all-gather.5
  125.7 213.5 all-reduce.1
  341.0 26.6 all-gather.7
  382.1 35.3 reduce-scatter.1
where the time goes:
time: 451 us; the launch traced here: 446 us
  waiting for transfers between devices  273 us (61%)
  matrix products  69.7 us (15%)
  local copies, waits for them, and re-layouts  57.5 us (13%)
  other arithmetic  30.2 us (7%)
  between operations  14.1 us (3%)
    psum x1, waiting for transfers between devices, body(): hidden_total = lax.psum(contract_last(sent_grad, w_out), 'gy')  185 us
    all_gather x1, waiting for transfers between devices, body(): lax.all_gather(pre_act, 'gy', axis=0, tiled=True).astype(jnp.float32)  59.1 us
    dot_general x2, matrix products, contract_last(): lax.dot_general(left, right, (((1,), (1,)), ((), ())), preferred_element_...  36 us
    dot_general x2, matrix products, token_sum(): lax.dot_general(left, right, (((0,), (0,)), ((), ())), preferred_element_...  33.7 us
    all_gather x1, waiting for transfers between devices, body(): lax.all_gather(out_grad, 'gx', axis=0, tiled=True)  27.9 us
    unnamed x1, local copies, waits for them, and re-layouts  21.3 us
    gather x1, local copies, waits for them, and re-layouts, body(): sent_pre = jnp.take(whole_pre, row_index, axis=0)  19.9 us
    scatter x1, local copies, waits for them, and re-layouts, body(): jnp.zeros((all_rows, sent_hidden.shape[1]), jnp.bfloat16).at[row_index]  14.2 us
  transfers between devices with their start and end apart: 5, of which 3 were waited for; matrix products, arithmetic and copies ran while one was open for 35% of the time, Pallas kernels for 0%

commit v1 on v0

v1 whole, which is shorter than its diff:
```python
import math

import jax
import jax.numpy as jnp
from jax import lax
from jax.experimental import pallas as pl
from jax.experimental.pallas import tpu as pltpu
from jax.sharding import PartitionSpec as P


CHUNKS = 4
MATMULS = ((0, 1), (1, 1), (2, 2))
bf16, f32 = jnp.bfloat16, jnp.float32
gelu_scale = math.sqrt(2.0 / math.pi)
cubic_coef = 0.044715


def gelu_value(pre):
    tangent = jnp.tanh(gelu_scale * (pre + cubic_coef * pre * pre * pre))
    return 0.5 * pre * (1.0 + tangent)


def gelu_slope(pre):
    tangent = jnp.tanh(gelu_scale * (pre + cubic_coef * pre * pre * pre))
    return 0.5 * (1.0 + tangent) + 0.5 * pre * (1.0 - tangent * tangent) * gelu_scale * (
        1.0 + 3.0 * cubic_coef * pre * pre
    )


def dot(left, right, over_left, over_right):
    return lax.dot_general(
        left, right, (((over_left,), (over_right,)), ((), ())), preferred_element_type=f32
    )


def cost(flops, bytes_accessed, transcendentals=0):
    return pl.CostEstimate(
        flops=flops, bytes_accessed=bytes_accessed, transcendentals=transcendentals
    )


def one_hot(slots, count):
    return (slots == lax.broadcasted_iota(jnp.int32, (slots.shape[0], count), 1)).astype(bf16)


def column(count):
    return lax.broadcasted_iota(jnp.int32, (count, 1), 0)


class Where:
    def __init__(self, table, rows, shards):
        self.chip, self.core, self.me_x = table[0], table[1], table[2]
        self.counts = [table[3 + s] for s in range(shards)]
        self.rows, self.shards = rows, shards
        self.half_live = rows * shards * 5 // 16

    def owner(self, count):
        place = column(count)
        second = (place >= self.half_live).astype(jnp.int32)
        packed = place - second * self.half_live
        packed = packed + jnp.bitwise_xor(second, self.core) * self.half_live
        owner, inner, end = jnp.zeros_like(packed), packed, 0
        for live in self.counts:
            end = end + live
            past = packed >= end
            owner = owner + past.astype(jnp.int32)
            inner = inner - jnp.where(past, live, 0)
        return owner, inner

    def gx_slot(self):
        owner, inner = self.owner(2 * self.half_live)
        return jnp.bitwise_xor(owner, self.me_x) * self.rows + inner

    def in_lanes(self, inner):
        lane = self.rows // 2
        upper = (inner >= lane).astype(jnp.int32)
        return jnp.bitwise_xor(upper, self.core) * lane + inner - upper * lane

    def pre_slot(self):
        owner, inner = self.owner(self.half_live)
        step = owner - self.chip
        group = jnp.where(step > 0, 2 * step - 1, -2 * step)
        group = jnp.where(jnp.abs(step) == self.shards // 2, self.shards - 1, group)
        return group * self.rows + self.in_lanes(inner)

    def live_count(self, shard):
        total = jnp.zeros_like(shard)
        for s, live in enumerate(self.counts):
            total = jnp.where(shard == s, live, total)
        return total

    def dy_slot(self, shifts):
        slots = []
        for shift in shifts:
            shard = self.chip + shift
            shard = jnp.where(shard >= self.shards, shard - self.shards, shard)
            inner = self.in_lanes(column(self.rows))
            slot = jnp.bitwise_xor(shard, self.me_x) * self.rows + inner
            slots.append(jnp.where(inner < self.live_count(shard), slot, -1))
        return jnp.concatenate(slots, axis=0)

    def unpack_slot(self):
        slots = []
        for s in range(self.shards):
            shard = jnp.bitwise_xor(self.me_x, s)
            begin = 0
            for other, live in enumerate(self.counts):
                begin = begin + jnp.where(other < shard, live, 0)
            inner = column(self.rows)
            packed = begin + inner
            second = (packed >= self.half_live).astype(jnp.int32)
            place = packed - second * self.half_live
            place = place + jnp.bitwise_xor(second, self.core) * self.half_live
            slots.append(jnp.where(inner < self.live_count(shard), place, -1))
        return jnp.concatenate(slots, axis=0)


SMEM = pl.BlockSpec(memory_space=pltpu.SMEM)


def stack(refs):
    return jnp.concatenate([r[...] for r in refs], axis=0)


def pick_rows(table, blocks, shifts):
    rows, model = blocks[0].shape
    shards = len(blocks)
    count = rows * shards
    live = count * 5 // 8

    def kernel(table_ref, *refs):
        where = Where(table_ref, rows, shards)
        packed, ordered = refs[shards:]
        tokens = stack(refs[:shards])
        packed[...] = dot(one_hot(where.gx_slot(), count), tokens, 1, 0).astype(bf16)
        ordered[...] = dot(one_hot(where.dy_slot(shifts), count), tokens, 1, 0).astype(bf16)

    return pl.pallas_call(
        kernel,
        in_specs=[SMEM] + [pl.BlockSpec((rows, model), lambda: (0, 0))] * shards,
        out_shape=[jax.ShapeDtypeStruct((n, model), bf16) for n in (live, count)],
        name="pick_rows",
        cost_estimate=cost(2 * (live + count) * count * model, 2 * (live + 2 * count) * model),
    )(table, *blocks)


def pick_columns(table, blocks):
    rows, model = blocks[0].shape
    shards = len(blocks)
    count = rows * shards
    live = count * 5 // 8

    def kernel(table_ref, *refs):
        hot = one_hot(Where(table_ref, rows, shards).gx_slot(), count)
        refs[-1][...] = dot(stack(refs[:-1]), hot, 0, 1).astype(bf16)

    return pl.pallas_call(
        kernel,
        in_specs=[SMEM] + [pl.BlockSpec((rows, model), lambda: (0, 0))] * shards,
        out_shape=jax.ShapeDtypeStruct((model, live), bf16),
        name="pick_columns",
        cost_estimate=cost(2 * live * count * model, 2 * (live + count) * model),
    )(table, *blocks)


def pick_wide(table, blocks, chunks):
    lane, width = blocks[0].shape
    count = lane * len(blocks)
    picked = count * 5 // 16
    tile = width // chunks

    def kernel(table_ref, *refs):
        ins, outs = refs[: len(blocks)], refs[len(blocks) :]
        hot = one_hot(Where(table_ref, 2 * lane, len(blocks) // 2).pre_slot(), count)
        rows = dot(hot, stack(ins), 1, 0).astype(bf16)
        for k, out in enumerate(outs):

            @pl.when(pl.program_id(0) == k)
            def _():
                out[...] = rows

    return pl.pallas_call(
        kernel,
        grid=(chunks,),
        in_specs=[SMEM] + [pl.BlockSpec((lane, tile), lambda i: (0, i))] * len(blocks),
        out_specs=[pl.BlockSpec((picked, tile), lambda i: (0, 0))] * chunks,
        out_shape=[jax.ShapeDtypeStruct((picked, tile), bf16)] * chunks,
        name="pick_wide",
        cost_estimate=cost(2 * picked * count * width, 2 * width * (picked + count)),
    )(table, *blocks)


def hidden_sums(dy, w_out, first, chunks, wide):
    live, model = dy.shape
    half = live // 2
    split = 2 if chunks == 1 else 1
    tile = wide // split

    def kernel(dy_ref, w_ref, *refs):
        part = dot(dy_ref[...], w_ref[...], 1, 1)
        if chunks == 1:
            refs[0][...] = part[:half]
            refs[1][...] = part[half:].astype(bf16)
            return
        for k in range(chunks):

            @pl.when(pl.program_id(0) == k)
            def _():
                refs[2 * k][...] = part[:half]
                refs[2 * k + 1][...] = part[half:].astype(bf16)

    at = (lambda i: (0, i)) if chunks == 1 else (lambda i: (0, 0))
    outs = pl.pallas_call(
        kernel,
        grid=(chunks * split,),
        in_specs=[
            pl.BlockSpec((live, model), lambda i: (0, 0)),
            pl.BlockSpec((tile, model), lambda i: (first * split + i, 0)),
        ],
        out_specs=[pl.BlockSpec((half, tile), at)] * (2 * chunks),
        out_shape=[jax.ShapeDtypeStruct((half, wide), t) for _ in range(chunks) for t in (f32, bf16)],
        name="hidden_sums",
        cost_estimate=cost(2 * live * model * wide * chunks, 2 * model * wide * chunks),
    )(dy, w_out)
    return list(zip(outs[::2], outs[1::2]))


def in_sum_of(lanes, mates, w_in, first):
    half, wide = lanes[0].shape
    model, chunks = w_in.shape[0], len(lanes)

    def kernel(*refs):
        w_ref, out = refs[2 * chunks :]
        for k in range(chunks):

            @pl.when(pl.program_id(0) == k)
            def _():
                hidden = stack([refs[k], refs[chunks + k]])
                part = dot(hidden, w_ref[...], 1, 1)
                out[...] = part if k == 0 else out[...] + part

    whole = pl.BlockSpec((half, wide), lambda i: (0, 0))
    return pl.pallas_call(
        kernel,
        grid=(chunks,),
        in_specs=[whole] * (2 * chunks) + [pl.BlockSpec((model, wide), lambda i: (0, first + i))],
        out_specs=pl.BlockSpec((2 * half, model), lambda i: (0, 0)),
        out_shape=jax.ShapeDtypeStruct((2 * half, model), f32),
        name="in_sum_of",
        cost_estimate=cost(4 * half * model * wide * chunks, 2 * model * wide * chunks),
    )(*lanes, *mates, w_in)


def in_last(table, lane, mate, w_in, at, before, rows, shards):
    half, wide = lane.shape
    model = w_in.shape[0]
    tile = wide // 2

    def kernel(table_ref, l_ref, m_ref, w_ref, before_ref, *refs):
        outs, acc = refs[:-1], refs[-1]
        part = dot(stack([l_ref, m_ref]), w_ref[...], 1, 1)

        @pl.when(pl.program_id(0) == 0)
        def _():
            acc[...] = before_ref[...] + part

        @pl.when(pl.program_id(0) == 1)
        def _():
            hot = one_hot(Where(table_ref, rows, shards).unpack_slot(), 2 * half)
            spread = dot(hot, (acc[...] + part).astype(bf16), 1, 0).astype(bf16)
            for s, out in enumerate(outs):
                out[...] = spread[s * rows : (s + 1) * rows]

    piece = pl.BlockSpec((half, tile), lambda i: (0, i))
    return pl.pallas_call(
        kernel,
        grid=(2,),
        in_specs=[
            SMEM,
            piece,
            piece,
            pl.BlockSpec((model, tile), lambda i: (0, 2 * at + i)),
            pl.BlockSpec((2 * half, model), lambda i: (0, 0)),
        ],
        out_specs=[pl.BlockSpec((rows, model), lambda i: (0, 0))] * shards,
        out_shape=[jax.ShapeDtypeStruct((rows, model), bf16)] * shards,
        scratch_shapes=[pltpu.VMEM((2 * half, model), f32)],
        name="in_last",
        cost_estimate=cost(4 * half * model * wide, 2 * model * wide + 12 * half * model),
    )(table, lane, mate, w_in, before)


def w_in_grad_of(x_t, lanes, mates):
    half, wide = lanes[0].shape
    model, live = x_t.shape
    chunks = len(lanes)

    def kernel(x_ref, *refs):
        for k in range(chunks):

            @pl.when(pl.program_id(0) == k)
            def _():
                hidden = stack([refs[k], refs[chunks + k]])
                refs[-1][...] = dot(x_ref[...], hidden, 1, 0).astype(bf16)

    whole = pl.BlockSpec((half, wide), lambda i: (0, 0))
    return pl.pallas_call(
        kernel,
        grid=(chunks,),
        in_specs=[pl.BlockSpec((model, live), lambda i: (0, 0))] + [whole] * (2 * chunks),
        out_specs=pl.BlockSpec((model, wide), lambda i: (0, i)),
        out_shape=jax.ShapeDtypeStruct((model, wide * chunks), bf16),
        name="w_in_grad_of",
        cost_estimate=cost(2 * live * model * wide * chunks, 2 * model * wide * chunks),
    )(x_t, *lanes, *mates)


def w_out_grad_of(flags, blocks, spare, dy, grad, first, tiles, tile):
    lane, width = blocks[0].shape
    tokens, model = dy.shape
    places = sorted(spare)

    def kernel(flag_ref, dy_ref, *refs):
        others = dict(zip(places, refs[len(blocks) :]))
        acts = []
        for k in range(len(blocks)):
            pre = refs[k][...].astype(f32)
            if k in others:
                pre = jnp.where(flag_ref[k] == 1, pre, others[k][...].astype(f32))
            acts.append(gelu_value(pre).astype(bf16))
        refs[-1][...] = dot(jnp.concatenate(acts, axis=0), dy_ref[...], 0, 0).astype(bf16)

    block = pl.BlockSpec((lane, tile), lambda i, flag: (0, first + i))
    specs = [pl.BlockSpec((tokens, model), lambda i, flag: (0, 0))]
    specs += [block] * (len(blocks) + len(places))
    operands = [flags, dy, *blocks, *[spare[k] for k in places]]
    aliases = {}
    if grad is not None:
        specs.append(pl.BlockSpec(memory_space=pl.ANY))
        aliases = {len(operands): 0}
        operands.append(grad)
    wide = tiles * tile
    return pl.pallas_call(
        kernel,
        grid_spec=pltpu.PrefetchScalarGridSpec(
            num_scalar_prefetch=1,
            grid=(tiles,),
            in_specs=specs,
            out_specs=pl.BlockSpec((tile, model), lambda i, flag: (first + i, 0)),
        ),
        out_shape=jax.ShapeDtypeStruct((width, model), bf16),
        input_output_aliases=aliases,
        name="w_out_grad_of",
        cost_estimate=cost(
            2 * tokens * model * wide, 2 * wide * (model + tokens), tokens * wide
        ),
    )(*operands)


def chip_pairs(pairs):
    return [(2 * a + c, 2 * b + c) for a, b in pairs for c in range(2)]


def backward(inputs, out_grad, pre_act, w_in, w_out, counts):
    shards = lax.axis_size("gx")
    chips = lax.axis_size("gy") // 2
    half = chips // 2
    rows = inputs.shape[0]
    lane = pre_act.shape[0]
    width = pre_act.shape[1]
    assert chips == shards and rows == 2 * lane
    me_x = lax.axis_index("gx")
    me_y = lax.axis_index("gy")
    chip, core = me_y // 2, me_y % 2

    def swap_cores(v):
        return lax.ppermute(v, "gy", [(k, k ^ 1) for k in range(2 * chips)])

    def swap_gx(v, s):
        return lax.ppermute(v, "gx", [(i, i ^ s) for i in range(shards)])

    def send(v, pairs):
        return lax.ppermute(v, "gy", chip_pairs(pairs))

    inward = [[(h, h + 1), (chips - 1 - h, chips - 2 - h)] for h in range(half - 1)]
    across = [(half - 1, half), (half, half - 1)]
    outward = [[(b, a) for a, b in pairs] for pairs in reversed(inward)]

    dy_blocks = [out_grad] + [swap_gx(out_grad, s) for s in range(1, shards)]
    x_blocks = [inputs] + [swap_gx(inputs, s) for s in range(1, shards)]

    plus, minus = {0: pre_act}, {0: pre_act}
    for k in range(1, half):
        plus[k] = send(plus[k - 1], [(z, z + 1) for z in range(k - 1, chips - 1)])
        minus[k] = send(minus[k - 1], [(z, z - 1) for z in range(1, chips - k + 1)])
    far = {}
    from_right = send(minus[half - 1], [(z, z - 1) for z in range(1, half + 1)])
    from_left = send(plus[half - 1], [(z, z + 1) for z in range(half - 1, chips - 1)])
    far[half] = jnp.where(chip >= half, from_left, from_right)
    for k in range(half + 1, chips):
        far[k] = send(
            far[k - 1],
            [(z, z - 1) for z in range(1, chips - k + 1)]
            + [(z, z + 1) for z in range(k - 1, chips - 1)],
        )

    def both(v):
        return [v, swap_cores(v)]

    blocks, spare, shifts, valid = both(pre_act), {}, [0], [1, 1]
    far2 = {k: both(far[k]) for k in range(half, chips)}
    for k in range(1, half):
        for near, shift, ok in (
            (both(minus[k]), k, chip + k < chips), (both(plus[k]), chips - k, chip >= k)
        ):
            spare[len(blocks)], spare[len(blocks) + 1] = far2[chips - k]
            blocks += near
            shifts.append(shift)
            valid += [ok.astype(jnp.int32)] * 2
    blocks += far2[half]
    shifts.append(half)
    valid += [1, 1]
    flags = jnp.stack([jnp.asarray(v, jnp.int32) for v in valid])

    table = jnp.concatenate([jnp.stack([chip, core, me_x]).astype(jnp.int32), counts])

    dy_packed, dy_ordered = pick_rows(table, dy_blocks, shifts)
    x_t = pick_columns(table, x_blocks)
    pre_packed = pick_wide(table, blocks, CHUNKS)

    wide = width // CHUNKS
    lanes, mates, parts = [], [], []
    for first, count in MATMULS:
        parts += hidden_sums(dy_packed, w_out, first, count, wide)
    for f in range(CHUNKS):
        total, sent = parts[f]
        got = swap_cores(sent)
        total = total + got.astype(f32)
        sent = lax.optimization_barrier(total.astype(bf16))
        for pairs in inward:
            got = send(sent, pairs)
            total = total + got.astype(f32)
            sent = lax.optimization_barrier(total.astype(bf16))
        got = send(sent, across)
        slope = gelu_slope(pre_packed[f].astype(f32))
        hidden = ((total + got.astype(f32)) * slope).astype(bf16)
        hidden = lax.optimization_barrier(hidden)
        for h, pairs in enumerate(outward):
            got = send(hidden, pairs)
            receivers = jnp.logical_or(chip == half - 2 - h, chip == half + 1 + h)
            hidden = jnp.where(receivers, got, hidden)
            hidden = lax.optimization_barrier(hidden)
        lanes.append(hidden)
        mates.append(swap_cores(hidden))

    tile = width // 4
    w_out_grad = w_out_grad_of(flags, blocks, spare, dy_ordered, None, 0, 2, tile)
    w_out_grad = w_out_grad_of(flags, blocks, spare, dy_ordered, w_out_grad, 2, 2, tile)
    in_sum = in_sum_of(lanes[:-1], mates[:-1], w_in, 0)
    spread = in_last(table, lanes[-1], mates[-1], w_in, CHUNKS - 1, in_sum, rows, shards)
    got = [swap_gx(spread[s], s) for s in range(1, shards)]
    w_in_grad = w_in_grad_of(x_t, lanes, mates)
    in_total = spread[0].astype(f32)
    for v in got:
        in_total = in_total + v.astype(f32)
    in_total = in_total.astype(bf16)
    return in_total, w_in_grad, w_out_grad


def solution(mesh):
    return jax.shard_map(
        backward,
        mesh=mesh,
        in_specs=(P("gx", "gy"), P("gx", "gy"), P("gy", "gx"), P("gy", "gx"), P("gx", "gy"), P()),
        out_specs=(P("gx", "gy"), P("gy", "gx"), P("gx", "gy")),
        check_vma=False,
    )
```

time: 451 us -> 280 us (0.62)
  waiting for transfers between devices: 273 us -> 121 us
  Pallas kernels: 0 us -> 84.7 us
  matrix products: 69.7 us -> 0 us
  local copies, waits for them, and re-layouts: 57.5 us -> 5.89 us
  starting transfers between devices: 0.72 us -> 44.1 us
  between operations: 14.1 us -> 1.31 us
  other arithmetic: 30.2 us -> 21.8 us
    psum x1 -> x0, waiting for transfers between devices: 185 us -> none  [body(): hidden_total = lax.psum(contract_last(sent_grad, w_out), 'gy')]
    ppermute x0 -> x39, waiting for transfers between devices: none -> 121 us  [the longest x17 110 us: send(): return lax.ppermute(v, 'gy', chip_pairs(pairs))]
    all_gather x3 -> x0, waiting for transfers between devices: 87 us -> none  [the longest x1 59.1 us: body(): lax.all_gather(pre_act, 'gy', axis=0, tiled=True).astype(jnp.float32)]
    pallas_call x0 -> x11, Pallas kernels: none -> 84.7 us  [the longest x2 24.9 us: w_out_grad_of(): pl.pallas_call(kernel, grid_spec=pltpu.PrefetchScalarGridSpec(num_scalar_...]
    dot_general x4 -> x0, matrix products: 69.7 us -> none  [the longest x2 36 us: contract_last(): lax.dot_general(left, right, (((1,), (1,)), ((), ())), preferred_element_...]
    ppermute x0 -> x39, starting transfers between devices: none -> 44.1 us  [the longest x17 31.7 us: send(): return lax.ppermute(v, 'gy', chip_pairs(pairs))]
    gather x2 -> x0, local copies, waits for them, and re-layouts: 22 us -> none  [the longest x1 19.9 us: body(): sent_pre = jnp.take(whole_pre, row_index, axis=0)]
    unnamed x1 -> x80, local copies, waits for them, and re-layouts: 21.3 us -> 5.31 us
  transfers between devices with their start and end apart: 5 -> 39, of which waited for: 3 -> 14; matrix products, arithmetic and copies ran while one was open for 35% -> 8% of each run, Pallas kernels for 0% -> 24%
where the time goes in v1:
time: 280 us; the launch traced here: 279 us
  waiting for transfers between devices  121 us (43%)
  Pallas kernels  84.7 us (30%)
  starting transfers between devices  44.1 us (16%)
  other arithmetic  21.8 us (8%)
  local copies, waits for them, and re-layouts  5.89 us (2%)
    ppermute x17, waiting for transfers between devices, send(): return lax.ppermute(v, 'gy', chip_pairs(pairs))  110 us
    ppermute x17, starting transfers between devices, send(): return lax.ppermute(v, 'gy', chip_pairs(pairs))  31.7 us
    pallas_call x2, Pallas kernels, w_out_grad_of(): pl.pallas_call(kernel, grid_spec=pltpu.PrefetchScalarGridSpec(num_scalar_...  24.9 us
    pallas_call x3, Pallas kernels, hidden_sums(): pl.pallas_call(kernel, grid=(chunks * split,), in_specs=[pl.BlockSpec((li...  16.8 us
    pallas_call x1, Pallas kernels, w_in_grad_of(): pl.pallas_call(kernel, grid=(chunks,), in_specs=[pl.BlockSpec((model, liv...  14.2 us
    ppermute x9, waiting for transfers between devices, swap_gx(): return lax.ppermute(v, 'gx', [(i, i ^ s) for i in range(shards)])  11.6 us
    ppermute x9, starting transfers between devices, swap_gx(): return lax.ppermute(v, 'gx', [(i, i ^ s) for i in range(shards)])  11.6 us
    convert_element_type x4, other arithmetic, backward(): hidden = ((total + got.astype(f32)) * slope).astype(bf16)  10.1 us
  transfers between devices with their start and end apart: 39, of which 14 were waited for; matrix products, arithmetic and copies ran while one was open for 8% of the time, Pallas kernels for 24%

profile of v1, /device:TPU:0, one launch (start us, length us, event | category | flops | bytes accessed | tf_op | source)
XLA Modules:
  0.0 278.9 jit_solution(3613989568633680878)
XLA Ops:
  6.5 4.6 %collective-permute-done.refs_1_ = bf16[128,1024]{1,0:T(8,128)(2,1)S(1)} collective-permute-done((bf16[128,1024]{1,0:T(8,128)(2,1)}, bf16[128,1024]{1,0:T(8,128)(2,1)S(1)}, u32[]{:S(2)}, u32[]{:S(2)}) %collective-permute-start) | collective-permute-done | bytes 262176 | tf_op jit(solution)/shard_map/ppermute | solution.py:380
  11.0 6.2 %collective-permute-done.1.refs_2_ = bf16[128,1024]{1,0:T(8,128)(2,1)S(1)} collective-permute-done((bf16[128,1024]{1,0:T(8,128)(2,1)}, bf16[128,1024]{1,0:T(8,128)(2,1)S(1)}, u32[]{:S(2)}, u32[]{:S(2)}) %collective-permute-start.1) | collective-permute-done | bytes 262176 | tf_op jit(solution)/shard_map/ppermute | solution.py:380
  22.0 7.8 %hidden_sums.3 = (f32[160,2048]{1,0:T(8,128)}, bf16[160,2048]{1,0:T(8,128)(2,1)}, f32[160,2048]{1,0:T(8,128)}, bf16[160,2048]{1,0:T(8,128)(2,1)}) custom-call(bf16[320,1024]{1,0:T(8,128)(2,1)} %get-tuple-element.21.dy_ref, bf16[8192,1024]{1,0:T(8,128)(2,1)} %w_ref.6), custom_call_target="tpu_custom_call" | custom-call | flops 2684354560 | bytes 8388608 | tf_op jit(solution)/shard_map/hidden_sums/pallas_call | solution.py:213
  33.3 4.5 %collective-permute-start.9 = (bf16[64,8192]{1,0:T(8,128)(2,1)S(1)}, bf16[64,8192]{1,0:T(8,128)(2,1)}, u32[]{:S(2)}, u32[]{:S(2)}) collective-permute-start(bf16[64,8192]{1,0:T(8,128)(2,1)S(1)} %copy-done.10), channel_id=1, source_target_pairs={{0,2},{1,3},{2,4},{3,5},{4,6},{5,7},{8,10},{9,11},{10,12},{11,13},... | collective-permute-start | bytes 3145736 | tf_op jit(solution)/shard_map/ppermute | solution.py:383
  38.4 4.5 %hidden_sums.5 = (f32[160,2048]{1,0:T(8,128)}, bf16[160,2048]{1,0:T(8,128)(2,1)}) custom-call(bf16[320,1024]{1,0:T(8,128)(2,1)} %get-tuple-element.21.dy_ref, bf16[8192,1024]{1,0:T(8,128)(2,1)} %w_ref.6), custom_call_target="tpu_custom_call" | custom-call | flops 1342177280 | bytes 4194304 | tf_op jit(solution)/shard_map/hidden_sums/pallas_call | solution.py:213
  48.7 4.6 %hidden_sums.4 = (f32[160,2048]{1,0:T(8,128)}, bf16[160,2048]{1,0:T(8,128)(2,1)}) custom-call(bf16[320,1024]{1,0:T(8,128)(2,1)} %get-tuple-element.21.dy_ref, bf16[8192,1024]{1,0:T(8,128)(2,1)} %w_ref.6), custom_call_target="tpu_custom_call" | custom-call | flops 1342177280 | bytes 4194304 | tf_op jit(solution)/shard_map/hidden_sums/pallas_call | solution.py:213
  56.5 4.1 %collective-permute-start.25 = (bf16[160,2048]{1,0:T(8,128)(2,1)S(1)}, bf16[160,2048]{1,0:T(8,128)(2,1)S(1)}, u32[]{:S(2)}, u32[]{:S(2)}) collective-permute-start(bf16[160,2048]{1,0:T(8,128)(2,1)S(1)} %fusion.39), channel_id=1, source_target_pairs={{0,2},{1,3},{6,4},{7,5},{8,10},{9,11},{14,12},{15,13},{16,18},{17,... | collective-permute-start | bytes 1966088 | tf_op jit(solution)/shard_map/ppermute | solution.py:383
  63.8 5.5 %collective-permute-done.7.refs_2_ = bf16[64,8192]{1,0:T(8,128)(2,1)} collective-permute-done((bf16[64,8192]{1,0:T(8,128)(2,1)S(1)}, bf16[64,8192]{1,0:T(8,128)(2,1)}, u32[]{:S(2)}, u32[]{:S(2)}) %collective-permute-start.7) | collective-permute-done | bytes 1048608 | tf_op jit(solution)/shard_map/ppermute | solution.py:383
  70.0 5.7 %collective-permute-done.25 = bf16[160,2048]{1,0:T(8,128)(2,1)S(1)} collective-permute-done((bf16[160,2048]{1,0:T(8,128)(2,1)S(1)}, bf16[160,2048]{1,0:T(8,128)(2,1)S(1)}, u32[]{:S(2)}, u32[]{:S(2)}) %collective-permute-start.25) | collective-permute-done | bytes 655392 | tf_op jit(solution)/shard_map/ppermute | solution.py:383
  78.1 11.6 %collective-permute-done.21 = bf16[160,2048]{1,0:T(8,128)(2,1)S(1)} collective-permute-done((bf16[160,2048]{1,0:T(8,128)(2,1)S(1)}, bf16[160,2048]{1,0:T(8,128)(2,1)S(1)}, u32[]{:S(2)}, u32[]{:S(2)}) %collective-permute-start.21) | collective-permute-done | bytes 655392 | tf_op jit(solution)/shard_map/ppermute | solution.py:383
  89.7 4.4 %collective-permute-start.4 = (bf16[160,2048]{1,0:T(8,128)(2,1)S(1)}, bf16[160,2048]{1,0:T(8,128)(2,1)S(1)}, u32[]{:S(2)}, u32[]{:S(2)}) collective-permute-start(bf16[160,2048]{1,0:T(8,128)(2,1)S(1)} %fusion.36), channel_id=1, source_target_pairs={{0,2},{1,3},{6,4},{7,5},{8,10},{9,11},{14,12},{15,13},{16,18},{17,... | collective-permute-start | bytes 1966088 | tf_op jit(solution)/shard_map/ppermute | solution.py:383
  96.4 5.7 %collective-permute-done.12 = bf16[64,8192]{1,0:T(8,128)(2,1)S(1)} collective-permute-done((bf16[64,8192]{1,0:T(8,128)(2,1)}, bf16[64,8192]{1,0:T(8,128)(2,1)S(1)}, u32[]{:S(2)}, u32[]{:S(2)}) %collective-permute-start.12) | collective-permute-done | bytes 1048608 | tf_op jit(solution)/shard_map/ppermute | solution.py:383
  104.9 12.1 %collective-permute-done.4 = bf16[160,2048]{1,0:T(8,128)(2,1)S(1)} collective-permute-done((bf16[160,2048]{1,0:T(8,128)(2,1)S(1)}, bf16[160,2048]{1,0:T(8,128)(2,1)S(1)}, u32[]{:S(2)}, u32[]{:S(2)}) %collective-permute-start.4) | collective-permute-done | bytes 655392 | tf_op jit(solution)/shard_map/ppermute | solution.py:383
  126.4 6.8 %pick_wide.1 = (bf16[160,2048]{1,0:T(8,128)(2,1)}, bf16[160,2048]{1,0:T(8,128)(2,1)}, bf16[160,2048]{1,0:T(8,128)(2,1)}, bf16[160,2048]{1,0:T(8,128)(2,1)}) custom-call(s32[7]{0:T(128)} %pad_add_fusion.table_ref, bf16[64,8192]{1,0:T(8,128)(2,1)} %refs_0_.9, bf16[64,8192]{1,0:T(8,128)(2,1)} %collective-permute-done.6.refs_1_, ...), custom_call_target="tpu_custom_call" | custom-call | flops 1342177280 | bytes 11010048 | tf_op jit(solution)/shard_map/pick_wide/pallas_call | solution.py:182
  149.0 15.6 %collective-permute-done.37.refs_8_.refs_10_ = bf16[64,8192]{1,0:T(8,128)(2,1)S(1)} collective-permute-done((bf16[64,8192]{1,0:T(8,128)(2,1)S(1)}, bf16[64,8192]{1,0:T(8,128)(2,1)S(1)}, u32[]{:S(2)}, u32[]{:S(2)}) %collective-permute-start.37) | collective-permute-done | bytes 1048608 | tf_op jit(solution)/shard_map/ppermute | solution.py:383
  164.6 14.0 %collective-permute-done.27 = bf16[160,2048]{1,0:T(8,128)(2,1)S(1)} collective-permute-done((bf16[160,2048]{1,0:T(8,128)(2,1)S(1)}, bf16[160,2048]{1,0:T(8,128)(2,1)S(1)}, u32[]{:S(2)}, u32[]{:S(2)}) %collective-permute-start.27) | collective-permute-done | bytes 655392 | tf_op jit(solution)/shard_map/ppermute | solution.py:383
  178.8 13.9 %collective-permute-done.23 = bf16[160,2048]{1,0:T(8,128)(2,1)S(1)} collective-permute-done((bf16[160,2048]{1,0:T(8,128)(2,1)S(1)}, bf16[160,2048]{1,0:T(8,128)(2,1)S(1)}, u32[]{:S(2)}, u32[]{:S(2)}) %collective-permute-start.23) | collective-permute-done | bytes 655392 | tf_op jit(solution)/shard_map/ppermute | solution.py:383
  192.9 13.9 %collective-permute-done.19 = bf16[160,2048]{1,0:T(8,128)(2,1)S(1)} collective-permute-done((bf16[160,2048]{1,0:T(8,128)(2,1)S(1)}, bf16[160,2048]{1,0:T(8,128)(2,1)S(1)}, u32[]{:S(2)}, u32[]{:S(2)}) %collective-permute-start.19) | collective-permute-done | bytes 655392 | tf_op jit(solution)/shard_map/ppermute | solution.py:383
  207.7 10.0 %collective-permute-done.14 = bf16[160,2048]{1,0:T(8,128)(2,1)S(1)} collective-permute-done((bf16[160,2048]{1,0:T(8,128)(2,1)S(1)}, bf16[160,2048]{1,0:T(8,128)(2,1)S(1)}, u32[]{:S(2)}, u32[]{:S(2)}) %collective-permute-start.14) | collective-permute-done | bytes 655392 | tf_op jit(solution)/shard_map/ppermute | solution.py:383
  219.6 12.7 %w_out_grad_of.2.refs_12_ = bf16[8192,1024]{1,0:T(8,128)(2,1)} custom-call(s32[8]{0:T(128)} %stack.33.flag_ref, bf16[512,1024]{1,0:T(8,128)(2,1)} %get-tuple-element.38.dy_ref, bf16[64,8192]{1,0:T(8,128)(2,1)} %refs_0_.9, bf16[64,8192]{1,0:T(8,128)(2,1)} %collective-permute-done.6.refs_1_, bf16[64,8192]{1,0:T(8,128)(2,1)} %collective-permute-done.7.refs_2_, ...), custom_call_target="tpu_custom_call" | custom-call | flops 4294967296 | bytes 12582912 | tf_op jit(solution)/shard_map/w_out_grad_of/pallas_call | solution.py:343
  232.3 12.2 %w_out_grad_of.3 = bf16[8192,1024]{1,0:T(8,128)(2,1)} custom-call(s32[8]{0:T(128)} %stack.33.flag_ref, bf16[512,1024]{1,0:T(8,128)(2,1)} %get-tuple-element.38.dy_ref, bf16[64,8192]{1,0:T(8,128)(2,1)} %refs_0_.9, bf16[64,8192]{1,0:T(8,128)(2,1)} %collective-permute-done.6.refs_1_, ...), custom_call_target="tpu_custom_call", output_to_operand_aliasing={{}: (14, {})} | custom-call | flops 4294967296 | bytes 12582912 | tf_op jit(solution)/shard_map/w_out_grad_of/pallas_call | solution.py:343
  244.6 9.7 %in_sum_of.1.before_ref = f32[320,1024]{1,0:T(8,128)} custom-call(bf16[160,2048]{1,0:T(8,128)(2,1)} %broadcast_select_fusion.3.refs_0_, bf16[160,2048]{1,0:T(8,128)(2,1)} %copy-done.15, bf16[160,2048]{1,0:T(8,128)(2,1)} %copy-done.14, bf16[160,2048]{1,0:T(8,128)(2,1)} %collective-permute-done.28.refs_3_.refs_4_, ...), custom_call_target="tpu_custom_call" | custom-call | flops 4026531840 | bytes 12582912 | tf_op jit(solution)/shard_map/in_sum_of/pallas_call | solution.py:243
  254.3 6.0 %in_last.1 = (bf16[128,1024]{1,0:T(8,128)(2,1)}, bf16[128,1024]{1,0:T(8,128)(2,1)}, bf16[128,1024]{1,0:T(8,128)(2,1)}, bf16[128,1024]{1,0:T(8,128)(2,1)}) custom-call(s32[7]{0:T(128)} %pad_add_fusion.table_ref, bf16[160,2048]{1,0:T(8,128)(2,1)} %broadcast_select_fusion.4.l_ref.refs_3_, bf16[160,2048]{1,0:T(8,128)(2,1)} %collective-permute-done.15.m_ref.refs_7_, ...), custom_call_target="tpu_custom_call" | custom-call | flops 1342177280 | bytes 6160384 | tf_op jit(solution)/shard_map/in_last/pallas_call | solution.py:275
  263.8 14.2 %w_in_grad_of.1 = bf16[1024,8192]{1,0:T(8,128)(2,1)} custom-call(bf16[1024,320]{1,0:T(8,128)(2,1)} %pick_columns.1.x_ref, bf16[160,2048]{1,0:T(8,128)(2,1)} %broadcast_select_fusion.3.refs_0_, bf16[160,2048]{1,0:T(8,128)(2,1)} %copy-done.15, bf16[160,2048]{1,0:T(8,128)(2,1)} %copy-done.14, bf16[160,2048]{1,0:T(8,128)(2,1)} %broadcast_select_fusion.4.l_ref.refs_3_, ...), custom_call_target="tpu_custom_call" | custom-call | flops 5368709120 | bytes 16777216 | tf_op jit(solution)/shard_map/w_in_grad_of/pallas_call | solution.py:307
  (166 shorter events, 67.4 us)
Async XLA Ops:
  29.8 23.6 %collective-permute-start.24 = (bf16[160,2048]{1,0:T(8,128)(2,1)}, bf16[160,2048]{1,0:T(8,128)(2,1)S(1)}, u32[]{:S(2)}, u32[]{:S(2)}) collective-permute-start(bf16[160,2048]{1,0:T(8,128)(2,1)} %get-tuple-element.32), channel_id=1, source_target_pairs={{0,1},{1,0},{2,3},{3,2},{4,5},{5,4},{6,7},{7,6},{8,9},{9,8},{10,11... | collective-permute-start | bytes 1966088 | tf_op jit(solution)/shard_map/ppermute | solution.py:377
  33.3 29.1 %collective-permute-start.9 = (bf16[64,8192]{1,0:T(8,128)(2,1)S(1)}, bf16[64,8192]{1,0:T(8,128)(2,1)}, u32[]{:S(2)}, u32[]{:S(2)}) collective-permute-start(bf16[64,8192]{1,0:T(8,128)(2,1)S(1)} %copy-done.10), channel_id=1, source_target_pairs={{0,2},{1,3},{2,4},{3,5},{4,6},{5,7},{8,10},{9,11},{10,12},{11,13},... | collective-permute-start | bytes 3145736 | tf_op jit(solution)/shard_map/ppermute | solution.py:383
  42.8 26.4 %collective-permute-start.7 = (bf16[64,8192]{1,0:T(8,128)(2,1)S(1)}, bf16[64,8192]{1,0:T(8,128)(2,1)}, u32[]{:S(2)}, u32[]{:S(2)}) collective-permute-start(bf16[64,8192]{1,0:T(8,128)(2,1)S(1)} %copy-done.10), channel_id=1, source_target_pairs={{2,0},{3,1},{4,2},{5,3},{6,4},{7,5},{10,8},{11,9},{12,10},{13,11},... | collective-permute-start | bytes 3145736 | tf_op jit(solution)/shard_map/ppermute | solution.py:383
  44.2 75.4 %collective-permute-start.6 = (bf16[64,8192]{1,0:T(8,128)(2,1)S(1)}, bf16[64,8192]{1,0:T(8,128)(2,1)}, u32[]{:S(2)}, u32[]{:S(2)}) collective-permute-start(bf16[64,8192]{1,0:T(8,128)(2,1)S(1)} %copy-done.10), channel_id=1, source_target_pairs={{0,1},{1,0},{2,3},{3,2},{4,5},{5,4},{6,7},{7,6},{8,9},{9,8},{10,11... | collective-permute-start | bytes 3145736 | tf_op jit(solution)/shard_map/ppermute | solution.py:377
  60.8 28.9 %collective-permute-start.21 = (bf16[160,2048]{1,0:T(8,128)(2,1)S(1)}, bf16[160,2048]{1,0:T(8,128)(2,1)S(1)}, u32[]{:S(2)}, u32[]{:S(2)}) collective-permute-start(bf16[160,2048]{1,0:T(8,128)(2,1)S(1)} %fusion.38), channel_id=1, source_target_pairs={{0,2},{1,3},{6,4},{7,5},{8,10},{9,11},{14,12},{15,13},{16,18},{17,... | collective-permute-start | bytes 1966088 | tf_op jit(solution)/shard_map/ppermute | solution.py:383
  62.4 41.3 %collective-permute-start.17 = (bf16[160,2048]{1,0:T(8,128)(2,1)S(1)}, bf16[160,2048]{1,0:T(8,128)(2,1)S(1)}, u32[]{:S(2)}, u32[]{:S(2)}) collective-permute-start(bf16[160,2048]{1,0:T(8,128)(2,1)S(1)} %fusion.37), channel_id=1, source_target_pairs={{0,2},{1,3},{6,4},{7,5},{8,10},{9,11},{14,12},{15,13},{16,18},{17,... | collective-permute-start | bytes 1966088 | tf_op jit(solution)/shard_map/ppermute | solution.py:383
  69.2 27.1 %collective-permute-start.11 = (bf16[64,8192]{1,0:T(8,128)(2,1)}, bf16[64,8192]{1,0:T(8,128)(2,1)S(1)}, u32[]{:S(2)}, u32[]{:S(2)}) collective-permute-start(bf16[64,8192]{1,0:T(8,128)(2,1)} %collective-permute-done.9.refs_4_), channel_id=1, source_target_pairs={{2,4},{3,5},{4,6},{5,7},{10,12},{11,13},{12,14},{13,15},{18,20},{1... | collective-permute-start | bytes 3145736 | tf_op jit(solution)/shard_map/ppermute | solution.py:383
  75.6 26.4 %collective-permute-start.12 = (bf16[64,8192]{1,0:T(8,128)(2,1)}, bf16[64,8192]{1,0:T(8,128)(2,1)S(1)}, u32[]{:S(2)}, u32[]{:S(2)}) collective-permute-start(bf16[64,8192]{1,0:T(8,128)(2,1)} %collective-permute-done.7.refs_2_), channel_id=1, source_target_pairs={{2,0},{3,1},{4,2},{5,3},{10,8},{11,9},{12,10},{13,11},{18,16},{19,... | collective-permute-start | bytes 3145736 | tf_op jit(solution)/shard_map/ppermute | solution.py:383
  89.7 27.3 %collective-permute-start.4 = (bf16[160,2048]{1,0:T(8,128)(2,1)S(1)}, bf16[160,2048]{1,0:T(8,128)(2,1)S(1)}, u32[]{:S(2)}, u32[]{:S(2)}) collective-permute-start(bf16[160,2048]{1,0:T(8,128)(2,1)S(1)} %fusion.36), channel_id=1, source_target_pairs={{0,2},{1,3},{6,4},{7,5},{8,10},{9,11},{14,12},{15,13},{16,18},{17,... | collective-permute-start | bytes 1966088 | tf_op jit(solution)/shard_map/ppermute | solution.py:383
  96.3 24.8 %collective-permute-start.10 = (bf16[64,8192]{1,0:T(8,128)(2,1)}, bf16[64,8192]{1,0:T(8,128)(2,1)S(1)}, u32[]{:S(2)}, u32[]{:S(2)}) collective-permute-start(bf16[64,8192]{1,0:T(8,128)(2,1)} %collective-permute-done.9.refs_4_), channel_id=1, source_target_pairs={{0,1},{1,0},{2,3},{3,2},{4,5},{5,4},{6,7},{7,6},{8,9},{9,8},{10,11... | collective-permute-start | bytes 3145736 | tf_op jit(solution)/shard_map/ppermute | solution.py:377
  102.1 20.6 %collective-permute-start.8 = (bf16[64,8192]{1,0:T(8,128)(2,1)}, bf16[64,8192]{1,0:T(8,128)(2,1)S(1)}, u32[]{:S(2)}, u32[]{:S(2)}) collective-permute-start(bf16[64,8192]{1,0:T(8,128)(2,1)} %collective-permute-done.7.refs_2_), channel_id=1, source_target_pairs={{0,1},{1,0},{2,3},{3,2},{4,5},{5,4},{6,7},{7,6},{8,9},{9,8},{10,11... | collective-permute-start | bytes 3145736 | tf_op jit(solution)/shard_map/ppermute | solution.py:377
  103.7 20.4 %collective-permute-start.13 = (bf16[64,8192]{1,0:T(8,128)(2,1)S(1)}, bf16[64,8192]{1,0:T(8,128)(2,1)S(1)}, u32[]{:S(2)}, u32[]{:S(2)}) collective-permute-start(bf16[64,8192]{1,0:T(8,128)(2,1)S(1)} %broadcast_select_fusion.refs_6_), channel_id=1, source_target_pairs={{0,1},{1,0},{2,3},{3,2},{4,5},{5,4},{6,7},{7,6},{8,9},{9,8},{10,11... | collective-permute-start | bytes 3145736 | tf_op jit(solution)/shard_map/ppermute | solution.py:377
  121.1 20.5 %collective-permute-start.18 = (bf16[160,2048]{1,0:T(8,128)(2,1)}, bf16[160,2048]{1,0:T(8,128)(2,1)}, u32[]{:S(2)}, u32[]{:S(2)}) collective-permute-start(bf16[160,2048]{1,0:T(8,128)(2,1)} %fusion.41), channel_id=1, source_target_pairs={{2,4},{3,5},{4,2},{5,3},{10,12},{11,13},{12,10},{13,11},{18,20},{1... | collective-permute-start | bytes 1966088 | tf_op jit(solution)/shard_map/ppermute | solution.py:383
  122.7 22.8 %collective-permute-start.5 = (bf16[160,2048]{1,0:T(8,128)(2,1)}, bf16[160,2048]{1,0:T(8,128)(2,1)}, u32[]{:S(2)}, u32[]{:S(2)}) collective-permute-start(bf16[160,2048]{1,0:T(8,128)(2,1)} %fusion.40), channel_id=1, source_target_pairs={{2,4},{3,5},{4,2},{5,3},{10,12},{11,13},{12,10},{13,11},{18,20},{1... | collective-permute-start | bytes 1966088 | tf_op jit(solution)/shard_map/ppermute | solution.py:383
  125.1 39.5 %collective-permute-start.37 = (bf16[64,8192]{1,0:T(8,128)(2,1)S(1)}, bf16[64,8192]{1,0:T(8,128)(2,1)S(1)}, u32[]{:S(2)}, u32[]{:S(2)}) collective-permute-start(bf16[64,8192]{1,0:T(8,128)(2,1)S(1)} %broadcast_select_fusion.refs_6_), channel_id=1, source_target_pairs={{2,0},{3,1},{4,6},{5,7},{10,8},{11,9},{12,14},{13,15},{18,16},{19,... | collective-permute-start | bytes 3145736 | tf_op jit(solution)/shard_map/ppermute | solution.py:383
  136.2 42.4 %collective-permute-start.27 = (bf16[160,2048]{1,0:T(8,128)(2,1)S(1)}, bf16[160,2048]{1,0:T(8,128)(2,1)S(1)}, u32[]{:S(2)}, u32[]{:S(2)}) collective-permute-start(bf16[160,2048]{1,0:T(8,128)(2,1)S(1)} %fusion.34), channel_id=1, source_target_pairs={{2,0},{3,1},{4,6},{5,7},{10,8},{11,9},{12,14},{13,15},{18,16},{19,... | collective-permute-start | bytes 1966088 | tf_op jit(solution)/shard_map/ppermute | solution.py:383
  140.4 52.3 %collective-permute-start.23 = (bf16[160,2048]{1,0:T(8,128)(2,1)S(1)}, bf16[160,2048]{1,0:T(8,128)(2,1)S(1)}, u32[]{:S(2)}, u32[]{:S(2)}) collective-permute-start(bf16[160,2048]{1,0:T(8,128)(2,1)S(1)} %fusion.25), channel_id=1, source_target_pairs={{2,0},{3,1},{4,6},{5,7},{10,8},{11,9},{12,14},{13,15},{18,16},{19,... | collective-permute-start | bytes 1966088 | tf_op jit(solution)/shard_map/ppermute | solution.py:383
  144.1 62.6 %collective-permute-start.19 = (bf16[160,2048]{1,0:T(8,128)(2,1)S(1)}, bf16[160,2048]{1,0:T(8,128)(2,1)S(1)}, u32[]{:S(2)}, u32[]{:S(2)}) collective-permute-start(bf16[160,2048]{1,0:T(8,128)(2,1)S(1)} %fusion.16), channel_id=1, source_target_pairs={{2,0},{3,1},{4,6},{5,7},{10,8},{11,9},{12,14},{13,15},{18,16},{19,... | collective-permute-start | bytes 1966088 | tf_op jit(solution)/shard_map/ppermute | solution.py:383
  147.7 70.0 %collective-permute-start.14 = (bf16[160,2048]{1,0:T(8,128)(2,1)S(1)}, bf16[160,2048]{1,0:T(8,128)(2,1)S(1)}, u32[]{:S(2)}, u32[]{:S(2)}) collective-permute-start(bf16[160,2048]{1,0:T(8,128)(2,1)S(1)} %fusion.7), channel_id=1, source_target_pairs={{2,0},{3,1},{4,6},{5,7},{10,8},{11,9},{12,14},{13,15},{18,16},{19,... | collective-permute-start | bytes 1966088 | tf_op jit(solution)/shard_map/ppermute | solution.py:383
  164.6 54.0 %collective-permute-start.38 = (bf16[64,8192]{1,0:T(8,128)(2,1)S(1)}, bf16[64,8192]{1,0:T(8,128)(2,1)S(1)}, u32[]{:S(2)}, u32[]{:S(2)}) collective-permute-start(bf16[64,8192]{1,0:T(8,128)(2,1)S(1)} %collective-permute-done.37.refs_8_.refs_10_), channel_id=1, source_target_pairs={{0,1},{1,0},{2,3},{3,2},{4,5},{5,4},{6,7},{7,6},{8,9},{9,8},{10,11... | collective-permute-start | bytes 3145736 | tf_op jit(solution)/shard_map/ppermute | solution.py:377
  178.7 65.8 %collective-permute-start.30 = (bf16[160,2048]{1,0:T(8,128)(2,1)S(1)}, bf16[160,2048]{1,0:T(8,128)(2,1)}, u32[]{:S(2)}, u32[]{:S(2)}) collective-permute-start(bf16[160,2048]{1,0:T(8,128)(2,1)S(1)} %broadcast_select_fusion.1.refs_2_), channel_id=1, source_target_pairs={{0,1},{1,0},{2,3},{3,2},{4,5},{5,4},{6,7},{7,6},{8,9},{9,8},{10,11... | collective-permute-start | bytes 1966088 | tf_op jit(solution)/shard_map/ppermute | solution.py:377
  192.8 51.8 %collective-permute-start.29 = (bf16[160,2048]{1,0:T(8,128)(2,1)S(1)}, bf16[160,2048]{1,0:T(8,128)(2,1)}, u32[]{:S(2)}, u32[]{:S(2)}) collective-permute-start(bf16[160,2048]{1,0:T(8,128)(2,1)S(1)} %broadcast_select_fusion.2.refs_1_), channel_id=1, source_target_pairs={{0,1},{1,0},{2,3},{3,2},{4,5},{5,4},{6,7},{7,6},{8,9},{9,8},{10,11... | collective-permute-start | bytes 1966088 | tf_op jit(solution)/shard_map/ppermute | solution.py:377
  207.7 36.9 %collective-permute-start.28 = (bf16[160,2048]{1,0:T(8,128)(2,1)}, bf16[160,2048]{1,0:T(8,128)(2,1)}, u32[]{:S(2)}, u32[]{:S(2)}) collective-permute-start(bf16[160,2048]{1,0:T(8,128)(2,1)} %broadcast_select_fusion.3.refs_0_), channel_id=1, source_target_pairs={{0,1},{1,0},{2,3},{3,2},{4,5},{5,4},{6,7},{7,6},{8,9},{9,8},{10,11... | collective-permute-start | bytes 1966088 | tf_op jit(solution)/shard_map/ppermute | solution.py:377
  218.6 35.7 %collective-permute-start.15 = (bf16[160,2048]{1,0:T(8,128)(2,1)}, bf16[160,2048]{1,0:T(8,128)(2,1)}, u32[]{:S(2)}, u32[]{:S(2)}) collective-permute-start(bf16[160,2048]{1,0:T(8,128)(2,1)} %broadcast_select_fusion.4.l_ref.refs_3_), channel_id=1, source_target_pairs={{0,1},{1,0},{2,3},{3,2},{4,5},{5,4},{6,7},{7,6},{8,9},{9,8},{10,11... | collective-permute-start | bytes 1966088 | tf_op jit(solution)/shard_map/ppermute | solution.py:377
  (55 other events, 574.1 us)

commit v2 on v1

--- a/solution.py
+++ b/solution.py
@@ -37,6 +37,10 @@
     return pl.CostEstimate(
         flops=flops, bytes_accessed=bytes_accessed, transcendentals=transcendentals
     )
+
+
+def vmem(mib):
+    return pltpu.CompilerParams(vmem_limit_bytes=mib << 20)
 
 
 def one_hot(slots, count):
@@ -140,6 +144,7 @@
         in_specs=[SMEM] + [pl.BlockSpec((rows, model), lambda: (0, 0))] * shards,
         out_shape=[jax.ShapeDtypeStruct((n, model), bf16) for n in (live, count)],
         name="pick_rows",
+        compiler_params=vmem(10),
         cost_estimate=cost(2 * (live + count) * count * model, 2 * (live + 2 * count) * model),
     )(table, *blocks)
 
@@ -159,6 +164,7 @@
         in_specs=[SMEM] + [pl.BlockSpec((rows, model), lambda: (0, 0))] * shards,
         out_shape=jax.ShapeDtypeStruct((model, live), bf16),
         name="pick_columns",
+        compiler_params=vmem(8),
         cost_estimate=cost(2 * live * count * model, 2 * (live + count) * model),
     )(table, *blocks)
 
@@ -186,6 +192,7 @@
         out_specs=[pl.BlockSpec((picked, tile), lambda i: (0, 0))] * chunks,
         out_shape=[jax.ShapeDtypeStruct((picked, tile), bf16)] * chunks,
         name="pick_wide",
+        compiler_params=vmem(14),
         cost_estimate=cost(2 * picked * count * width, 2 * width * (picked + count)),
     )(table, *blocks)
 
@@ -220,6 +227,7 @@
         out_specs=[pl.BlockSpec((half, tile), at)] * (2 * chunks),
         out_shape=[jax.ShapeDtypeStruct((half, wide), t) for _ in range(chunks) for t in (f32, bf16)],
         name="hidden_sums",
+        compiler_params=vmem(12 if chunks == 1 else 22),
         cost_estimate=cost(2 * live * model * wide * chunks, 2 * model * wide * chunks),
     )(dy, w_out)
     return list(zip(outs[::2], outs[1::2]))
@@ -247,6 +255,7 @@
         out_specs=pl.BlockSpec((2 * half, model), lambda i: (0, 0)),
         out_shape=jax.ShapeDtypeStruct((2 * half, model), f32),
         name="in_sum_of",
+        compiler_params=vmem(22),
         cost_estimate=cost(4 * half * model * wide * chunks, 2 * model * wide * chunks),
     )(*lanes, *mates, w_in)
 
@@ -286,6 +295,7 @@
         out_shape=[jax.ShapeDtypeStruct((rows, model), bf16)] * shards,
         scratch_shapes=[pltpu.VMEM((2 * half, model), f32)],
         name="in_last",
+        compiler_params=vmem(16),
         cost_estimate=cost(4 * half * model * wide, 2 * model * wide + 12 * half * model),
     )(table, lane, mate, w_in, before)
 
@@ -311,6 +321,7 @@
         out_specs=pl.BlockSpec((model, wide), lambda i: (0, i)),
         out_shape=jax.ShapeDtypeStruct((model, wide * chunks), bf16),
         name="w_in_grad_of",
+        compiler_params=vmem(22),
         cost_estimate=cost(2 * live * model * wide * chunks, 2 * model * wide * chunks),
     )(x_t, *lanes, *mates)
 
@@ -351,6 +362,7 @@
         out_shape=jax.ShapeDtypeStruct((width, model), bf16),
         input_output_aliases=aliases,
         name="w_out_grad_of",
+        compiler_params=vmem(28),
         cost_estimate=cost(
             2 * tokens * model * wide, 2 * wide * (model + tokens), tokens * wide
         ),
@@ -453,9 +465,9 @@
         lanes.append(hidden)
         mates.append(swap_cores(hidden))
 
-    tile = width // 4
-    w_out_grad = w_out_grad_of(flags, blocks, spare, dy_ordered, None, 0, 2, tile)
-    w_out_grad = w_out_grad_of(flags, blocks, spare, dy_ordered, w_out_grad, 2, 2, tile)
+    tile = width // 8
+    w_out_grad = w_out_grad_of(flags, blocks, spare, dy_ordered, None, 0, 4, tile)
+    w_out_grad = w_out_grad_of(flags, blocks, spare, dy_ordered, w_out_grad, 4, 4, tile)
     in_sum = in_sum_of(lanes[:-1], mates[:-1], w_in, 0)
     spread = in_last(table, lanes[-1], mates[-1], w_in, CHUNKS - 1, in_sum, rows, shards)
     got = [swap_gx(spread[s], s) for s in range(1, shards)]

time: 280 us -> 269 us (0.961)
  Pallas kernels: 84.7 us -> 58.4 us
  waiting for transfers between devices: 121 us -> 138 us
  other arithmetic: 21.8 us -> 11.5 us
  local copies, waits for them, and re-layouts: 5.89 us -> 14.4 us
    ppermute x17, waiting for transfers between devices: 110 us -> 126 us  [send(): return lax.ppermute(v, 'gy', chip_pairs(pairs))]
    unnamed x80 -> x24, local copies, waits for them, and re-layouts: 5.31 us -> 14.3 us
    pallas_call x3, Pallas kernels: 16.8 us -> 8.01 us  [hidden_sums(): pl.pallas_call(kernel, grid=(chunks * split,), in_specs=[pl.BlockSpec((li...]
    convert_element_type x4, other arithmetic: 10.1 us -> 5.66 us  [backward(): hidden = ((total + got.astype(f32)) * slope).astype(bf16)]
    pallas_call x1, Pallas kernels: 9.71 us -> 5.56 us  [in_sum_of(): pl.pallas_call(kernel, grid=(chunks,), in_specs=[whole] * (2 * chunks) +...]
    convert_element_type x8, other arithmetic: 7.35 us -> 3.89 us  [backward(): sent = lax.optimization_barrier(total.astype(bf16))]
    pallas_call x2, Pallas kernels: 24.9 us -> 21.9 us  [w_out_grad_of(): pl.pallas_call(kernel, grid_spec=pltpu.PrefetchScalarGridSpec(num_scalar_...]
  transfers between devices with their start and end apart: 39 -> 39, of which waited for: 14 -> 15; matrix products, arithmetic and copies ran while one was open for 8% -> 4% of each run, Pallas kernels for 24% -> 18%
where the time goes in v2:
time: 269 us; the launch traced here: 268 us
  waiting for transfers between devices  138 us (51%)
  Pallas kernels  58.4 us (22%)
  starting transfers between devices  45.2 us (17%)
  local copies, waits for them, and re-layouts  14.4 us (5%)
  other arithmetic  11.5 us (4%)
    ppermute x17, waiting for transfers between devices, send(): return lax.ppermute(v, 'gy', chip_pairs(pairs))  126 us
    ppermute x17, starting transfers between devices, send(): return lax.ppermute(v, 'gy', chip_pairs(pairs))  32 us
    pallas_call x2, Pallas kernels, w_out_grad_of(): pl.pallas_call(kernel, grid_spec=pltpu.PrefetchScalarGridSpec(num_scalar_...  21.9 us
    unnamed x24, local copies, waits for them, and re-layouts  14.3 us
    ppermute x9, starting transfers between devices, swap_gx(): return lax.ppermute(v, 'gx', [(i, i ^ s) for i in range(shards)])  11.6 us
    ppermute x9, waiting for transfers between devices, swap_gx(): return lax.ppermute(v, 'gx', [(i, i ^ s) for i in range(shards)])  11.6 us
    pallas_call x1, Pallas kernels, w_in_grad_of(): pl.pallas_call(kernel, grid=(chunks,), in_specs=[pl.BlockSpec((model, liv...  11.5 us
    pallas_call x3, Pallas kernels, hidden_sums(): pl.pallas_call(kernel, grid=(chunks * split,), in_specs=[pl.BlockSpec((li...  8.01 us
  transfers between devices with their start and end apart: 39, of which 15 were waited for; matrix products, arithmetic and copies ran while one was open for 4% of the time, Pallas kernels for 18%

profile of v2, /device:TPU:0, one launch (start us, length us, event | category | flops | bytes accessed | tf_op | source)
XLA Modules:
  0.0 268.3 jit_solution(5985394355138280632)
XLA Ops:
  5.9 5.1 %collective-permute-done.refs_1_ = bf16[128,1024]{1,0:T(8,128)(2,1)S(1)} collective-permute-done((bf16[128,1024]{1,0:T(8,128)(2,1)}, bf16[128,1024]{1,0:T(8,128)(2,1)S(1)}, u32[]{:S(2)}, u32[]{:S(2)}) %collective-permute-start) | collective-permute-done | bytes 262176 | tf_op jit(solution)/shard_map/ppermute | solution.py:392
  11.0 6.2 %collective-permute-done.1.refs_2_ = bf16[128,1024]{1,0:T(8,128)(2,1)S(1)} collective-permute-done((bf16[128,1024]{1,0:T(8,128)(2,1)}, bf16[128,1024]{1,0:T(8,128)(2,1)S(1)}, u32[]{:S(2)}, u32[]{:S(2)}) %collective-permute-start.1) | collective-permute-done | bytes 262176 | tf_op jit(solution)/shard_map/ppermute | solution.py:392
  20.9 5.8 %copy-done = bf16[8192,1024]{1,0:T(8,128)(2,1)S(1)} copy-done((bf16[8192,1024]{1,0:T(8,128)(2,1)S(1)}, bf16[8192,1024]{1,0:T(8,128)(2,1)}, u32[]{:S(2)}) %copy-start) | copy-done | bytes 16777240
  26.6 4.2 %hidden_sums.3 = (f32[160,2048]{1,0:T(8,128)S(1)}, bf16[160,2048]{1,0:T(8,128)(2,1)}, f32[160,2048]{1,0:T(8,128)S(1)}, bf16[160,2048]{1,0:T(8,128)(2,1)S(1)}) custom-call(bf16[320,1024]{1,0:T(8,128)(2,1)S(1)} %get-tuple-element.21.dy_ref, bf16[8192,1024]{1,0:T(8,128)(2,1)S(1)} %copy-done), custom_call_target="tpu_custom_call" | custom-call | flops 2684354560 | bytes 8388608 | tf_op jit(solution)/shard_map/hidden_sums/pallas_call | solution.py:220
  35.2 4.5 %collective-permute-start.9 = (bf16[64,8192]{1,0:T(8,128)(2,1)}, bf16[64,8192]{1,0:T(8,128)(2,1)}, u32[]{:S(2)}, u32[]{:S(2)}) collective-permute-start(bf16[64,8192]{1,0:T(8,128)(2,1)} %refs_0_.9), channel_id=1, source_target_pairs={{0,2},{1,3},{2,4},{3,5},{4,6},{5,7},{8,10},{9,11},{10,12},{11,13},... | collective-permute-start | bytes 3145736 | tf_op jit(solution)/shard_map/ppermute | solution.py:395
  39.8 5.8 %copy-done.1 = bf16[8192,1024]{1,0:T(8,128)(2,1)S(1)} copy-done((bf16[8192,1024]{1,0:T(8,128)(2,1)S(1)}, bf16[8192,1024]{1,0:T(8,128)(2,1)}, u32[]{:S(2)}) %copy-start.1) | copy-done | bytes 16777240
  55.4 4.6 %collective-permute-start.25 = (bf16[160,2048]{1,0:T(8,128)(2,1)S(1)}, bf16[160,2048]{1,0:T(8,128)(2,1)S(1)}, u32[]{:S(2)}, u32[]{:S(2)}) collective-permute-start(bf16[160,2048]{1,0:T(8,128)(2,1)S(1)} %fusion.39), channel_id=1, source_target_pairs={{0,2},{1,3},{6,4},{7,5},{8,10},{9,11},{14,12},{15,13},{16,18},{17,... | collective-permute-start | bytes 1966088 | tf_op jit(solution)/shard_map/ppermute | solution.py:395
  62.2 4.4 %collective-permute-start.17 = (bf16[160,2048]{1,0:T(8,128)(2,1)S(1)}, bf16[160,2048]{1,0:T(8,128)(2,1)S(1)}, u32[]{:S(2)}, u32[]{:S(2)}) collective-permute-start(bf16[160,2048]{1,0:T(8,128)(2,1)S(1)} %fusion.37), channel_id=1, source_target_pairs={{0,2},{1,3},{6,4},{7,5},{8,10},{9,11},{14,12},{15,13},{16,18},{17,... | collective-permute-start | bytes 1966088 | tf_op jit(solution)/shard_map/ppermute | solution.py:395
  66.6 7.4 %collective-permute-done.7.refs_2_ = bf16[64,8192]{1,0:T(8,128)(2,1)S(1)} collective-permute-done((bf16[64,8192]{1,0:T(8,128)(2,1)}, bf16[64,8192]{1,0:T(8,128)(2,1)S(1)}, u32[]{:S(2)}, u32[]{:S(2)}) %collective-permute-start.7) | collective-permute-done | bytes 1048608 | tf_op jit(solution)/shard_map/ppermute | solution.py:395
  78.8 11.4 %collective-permute-done.21 = bf16[160,2048]{1,0:T(8,128)(2,1)S(1)} collective-permute-done((bf16[160,2048]{1,0:T(8,128)(2,1)S(1)}, bf16[160,2048]{1,0:T(8,128)(2,1)S(1)}, u32[]{:S(2)}, u32[]{:S(2)}) %collective-permute-start.21) | collective-permute-done | bytes 655392 | tf_op jit(solution)/shard_map/ppermute | solution.py:395
  90.2 4.4 %collective-permute-start.4 = (bf16[160,2048]{1,0:T(8,128)(2,1)S(1)}, bf16[160,2048]{1,0:T(8,128)(2,1)S(1)}, u32[]{:S(2)}, u32[]{:S(2)}) collective-permute-start(bf16[160,2048]{1,0:T(8,128)(2,1)S(1)} %fusion.36), channel_id=1, source_target_pairs={{0,2},{1,3},{6,4},{7,5},{8,10},{9,11},{14,12},{15,13},{16,18},{17,... | collective-permute-start | bytes 1966088 | tf_op jit(solution)/shard_map/ppermute | solution.py:395
  95.0 7.0 %collective-permute-done.12 = bf16[64,8192]{1,0:T(8,128)(2,1)S(1)} collective-permute-done((bf16[64,8192]{1,0:T(8,128)(2,1)S(1)}, bf16[64,8192]{1,0:T(8,128)(2,1)S(1)}, u32[]{:S(2)}, u32[]{:S(2)}) %collective-permute-start.12) | collective-permute-done | bytes 1048608 | tf_op jit(solution)/shard_map/ppermute | solution.py:395
  104.5 12.8 %collective-permute-done.4 = bf16[160,2048]{1,0:T(8,128)(2,1)S(1)} collective-permute-done((bf16[160,2048]{1,0:T(8,128)(2,1)S(1)}, bf16[160,2048]{1,0:T(8,128)(2,1)S(1)}, u32[]{:S(2)}, u32[]{:S(2)}) %collective-permute-start.4) | collective-permute-done | bytes 655392 | tf_op jit(solution)/shard_map/ppermute | solution.py:395
  121.7 4.3 %pick_wide.1 = (bf16[160,2048]{1,0:T(8,128)(2,1)S(1)}, bf16[160,2048]{1,0:T(8,128)(2,1)S(1)}, bf16[160,2048]{1,0:T(8,128)(2,1)S(1)}, bf16[160,2048]{1,0:T(8,128)(2,1)S(1)}) custom-call(s32[7]{0:T(128)S(1)} %pad_add_fusion.table_ref, bf16[64,8192]{1,0:T(8,128)(2,1)} %refs_0_.9, bf16[64,8192]{1,0:T(8,128)(2,1)S(1)} %collective-permute-done.6.refs_1_, ...), custom_call_target="tpu_custom_call" | custom-call | flops 1342177280 | bytes 11010048 | tf_op jit(solution)/shard_map/pick_wide/pallas_call | solution.py:188
  137.2 30.5 %collective-permute-done.37.refs_8_.refs_10_ = bf16[64,8192]{1,0:T(8,128)(2,1)S(1)} collective-permute-done((bf16[64,8192]{1,0:T(8,128)(2,1)S(1)}, bf16[64,8192]{1,0:T(8,128)(2,1)S(1)}, u32[]{:S(2)}, u32[]{:S(2)}) %collective-permute-start.37) | collective-permute-done | bytes 1048608 | tf_op jit(solution)/shard_map/ppermute | solution.py:395
  167.7 14.0 %collective-permute-done.27 = bf16[160,2048]{1,0:T(8,128)(2,1)S(1)} collective-permute-done((bf16[160,2048]{1,0:T(8,128)(2,1)S(1)}, bf16[160,2048]{1,0:T(8,128)(2,1)S(1)}, u32[]{:S(2)}, u32[]{:S(2)}) %collective-permute-start.27) | collective-permute-done | bytes 655392 | tf_op jit(solution)/shard_map/ppermute | solution.py:395
  181.8 13.9 %collective-permute-done.23 = bf16[160,2048]{1,0:T(8,128)(2,1)S(1)} collective-permute-done((bf16[160,2048]{1,0:T(8,128)(2,1)S(1)}, bf16[160,2048]{1,0:T(8,128)(2,1)S(1)}, u32[]{:S(2)}, u32[]{:S(2)}) %collective-permute-start.23) | collective-permute-done | bytes 655392 | tf_op jit(solution)/shard_map/ppermute | solution.py:395
  195.9 13.9 %collective-permute-done.19 = bf16[160,2048]{1,0:T(8,128)(2,1)S(1)} collective-permute-done((bf16[160,2048]{1,0:T(8,128)(2,1)S(1)}, bf16[160,2048]{1,0:T(8,128)(2,1)S(1)}, u32[]{:S(2)}, u32[]{:S(2)}) %collective-permute-start.19) | collective-permute-done | bytes 655392 | tf_op jit(solution)/shard_map/ppermute | solution.py:395
  209.9 10.9 %collective-permute-done.14 = bf16[160,2048]{1,0:T(8,128)(2,1)S(1)} collective-permute-done((bf16[160,2048]{1,0:T(8,128)(2,1)S(1)}, bf16[160,2048]{1,0:T(8,128)(2,1)S(1)}, u32[]{:S(2)}, u32[]{:S(2)}) %collective-permute-start.14) | collective-permute-done | bytes 655392 | tf_op jit(solution)/shard_map/ppermute | solution.py:395
  221.0 11.0 %w_out_grad_of.2.refs_12_ = bf16[8192,1024]{1,0:T(8,128)(2,1)} custom-call(s32[8]{0:T(128)S(1)} %stack.33.flag_ref, bf16[512,1024]{1,0:T(8,128)(2,1)S(1)} %copy-done.3, bf16[64,8192]{1,0:T(8,128)(2,1)} %refs_0_.9, bf16[64,8192]{1,0:T(8,128)(2,1)S(1)} %collective-permute-done.6.refs_1_, bf16[64,8192]{1,0:T(8,128)(2,1)S(1)} %collective-permute-done.7.refs_2_, ...), custom_call_target="tpu_custom_call" | custom-call | flops 4294967296 | bytes 12582912 | tf_op jit(solution)/shard_map/w_out_grad_of/pallas_call | solution.py:354
  232.0 11.0 %w_out_grad_of.3 = bf16[8192,1024]{1,0:T(8,128)(2,1)} custom-call(s32[8]{0:T(128)S(1)} %stack.33.flag_ref, bf16[512,1024]{1,0:T(8,128)(2,1)S(1)} %copy-done.3, bf16[64,8192]{1,0:T(8,128)(2,1)} %refs_0_.9, bf16[64,8192]{1,0:T(8,128)(2,1)S(1)} %collective-permute-done.6.refs_1_, ...), custom_call_target="tpu_custom_call", output_to_operand_aliasing={{}: (14, {})} | custom-call | flops 4294967296 | bytes 12582912 | tf_op jit(solution)/shard_map/w_out_grad_of/pallas_call | solution.py:354
  243.0 5.6 %in_sum_of.1.before_ref = f32[320,1024]{1,0:T(8,128)S(1)} custom-call(bf16[160,2048]{1,0:T(8,128)(2,1)S(1)} %broadcast_select_fusion.3.refs_0_, bf16[160,2048]{1,0:T(8,128)(2,1)S(1)} %broadcast_select_fusion.2.refs_1_, bf16[160,2048]{1,0:T(8,128)(2,1)S(1)} %broadcast_select_fusion.1.refs_2_, bf16[160,2048]{1,0:T(8,128)(2,1)S(1)} %collective-permute-done.28.refs_3_.refs_4_, ...), custom_call_target="tpu_custom_call" | custom-call | flops 4026531840 | bytes 12582912 | tf_op jit(solution)/shard_map/in_sum_of/pallas_call | solution.py:251
  248.6 3.5 %in_last.1 = (bf16[128,1024]{1,0:T(8,128)(2,1)S(1)}, bf16[128,1024]{1,0:T(8,128)(2,1)S(1)}, bf16[128,1024]{1,0:T(8,128)(2,1)S(1)}, bf16[128,1024]{1,0:T(8,128)(2,1)S(1)}) custom-call(s32[7]{0:T(128)S(1)} %pad_add_fusion.table_ref, bf16[160,2048]{1,0:T(8,128)(2,1)S(1)} %broadcast_select_fusion.4.l_ref.refs_3_, ...), custom_call_target="tpu_custom_call" | custom-call | flops 1342177280 | bytes 6160384 | tf_op jit(solution)/shard_map/in_last/pallas_call | solution.py:284
  255.7 11.5 %w_in_grad_of.1 = bf16[1024,8192]{1,0:T(8,128)(2,1)} custom-call(bf16[1024,320]{1,0:T(8,128)(2,1)S(1)} %pick_columns.1.x_ref, bf16[160,2048]{1,0:T(8,128)(2,1)S(1)} %broadcast_select_fusion.3.refs_0_, bf16[160,2048]{1,0:T(8,128)(2,1)S(1)} %broadcast_select_fusion.2.refs_1_, bf16[160,2048]{1,0:T(8,128)(2,1)S(1)} %broadcast_select_fusion.1.refs_2_, ...), custom_call_target="tpu_custom_call" | custom-call | flops 5368709120 | bytes 16777216 | tf_op jit(solution)/shard_map/w_in_grad_of/pallas_call | solution.py:317
  (111 shorter events, 53.5 us)
Async XLA Ops:
  31.7 21.5 %collective-permute-start.24 = (bf16[160,2048]{1,0:T(8,128)(2,1)}, bf16[160,2048]{1,0:T(8,128)(2,1)}, u32[]{:S(2)}, u32[]{:S(2)}) collective-permute-start(bf16[160,2048]{1,0:T(8,128)(2,1)} %get-tuple-element.32), channel_id=1, source_target_pairs={{0,1},{1,0},{2,3},{3,2},{4,5},{5,4},{6,7},{7,6},{8,9},{9,8},{10,11... | collective-permute-start | bytes 1966088 | tf_op jit(solution)/shard_map/ppermute | solution.py:389
  32.9 15.8 %collective-permute-start.35 = (bf16[128,1024]{1,0:T(8,128)(2,1)S(1)}, bf16[128,1024]{1,0:T(8,128)(2,1)}, u32[]{:S(2)}, u32[]{:S(2)}) collective-permute-start(bf16[128,1024]{1,0:T(8,128)(2,1)S(1)} %copy-done.4), channel_id=1, source_target_pairs={{0,16},{8,24},{16,0},{24,8},{1,17},{9,25},{17,1},{25,9},{2,18},{10... | collective-permute-start | bytes 786440 | tf_op jit(solution)/shard_map/ppermute | solution.py:392
  35.2 27.0 %collective-permute-start.9 = (bf16[64,8192]{1,0:T(8,128)(2,1)}, bf16[64,8192]{1,0:T(8,128)(2,1)}, u32[]{:S(2)}, u32[]{:S(2)}) collective-permute-start(bf16[64,8192]{1,0:T(8,128)(2,1)} %refs_0_.9), channel_id=1, source_target_pairs={{0,2},{1,3},{2,4},{3,5},{4,6},{5,7},{8,10},{9,11},{10,12},{11,13},... | collective-permute-start | bytes 3145736 | tf_op jit(solution)/shard_map/ppermute | solution.py:395
  47.4 26.6 %collective-permute-start.7 = (bf16[64,8192]{1,0:T(8,128)(2,1)}, bf16[64,8192]{1,0:T(8,128)(2,1)S(1)}, u32[]{:S(2)}, u32[]{:S(2)}) collective-permute-start(bf16[64,8192]{1,0:T(8,128)(2,1)} %refs_0_.9), channel_id=1, source_target_pairs={{2,0},{3,1},{4,2},{5,3},{6,4},{7,5},{10,8},{11,9},{12,10},{13,11},... | collective-permute-start | bytes 3145736 | tf_op jit(solution)/shard_map/ppermute | solution.py:395
  48.8 69.5 %collective-permute-start.6 = (bf16[64,8192]{1,0:T(8,128)(2,1)}, bf16[64,8192]{1,0:T(8,128)(2,1)S(1)}, u32[]{:S(2)}, u32[]{:S(2)}) collective-permute-start(bf16[64,8192]{1,0:T(8,128)(2,1)} %refs_0_.9), channel_id=1, source_target_pairs={{0,1},{1,0},{2,3},{3,2},{4,5},{5,4},{6,7},{7,6},{8,9},{9,8},{10,11... | collective-permute-start | bytes 3145736 | tf_op jit(solution)/shard_map/ppermute | solution.py:389
  55.4 20.8 %collective-permute-start.25 = (bf16[160,2048]{1,0:T(8,128)(2,1)S(1)}, bf16[160,2048]{1,0:T(8,128)(2,1)S(1)}, u32[]{:S(2)}, u32[]{:S(2)}) collective-permute-start(bf16[160,2048]{1,0:T(8,128)(2,1)S(1)} %fusion.39), channel_id=1, source_target_pairs={{0,2},{1,3},{6,4},{7,5},{8,10},{9,11},{14,12},{15,13},{16,18},{17,... | collective-permute-start | bytes 1966088 | tf_op jit(solution)/shard_map/ppermute | solution.py:395
  60.1 30.1 %collective-permute-start.21 = (bf16[160,2048]{1,0:T(8,128)(2,1)S(1)}, bf16[160,2048]{1,0:T(8,128)(2,1)S(1)}, u32[]{:S(2)}, u32[]{:S(2)}) collective-permute-start(bf16[160,2048]{1,0:T(8,128)(2,1)S(1)} %fusion.38), channel_id=1, source_target_pairs={{0,2},{1,3},{6,4},{7,5},{8,10},{9,11},{14,12},{15,13},{16,18},{17,... | collective-permute-start | bytes 1966088 | tf_op jit(solution)/shard_map/ppermute | solution.py:395
  62.2 42.0 %collective-permute-start.17 = (bf16[160,2048]{1,0:T(8,128)(2,1)S(1)}, bf16[160,2048]{1,0:T(8,128)(2,1)S(1)}, u32[]{:S(2)}, u32[]{:S(2)}) collective-permute-start(bf16[160,2048]{1,0:T(8,128)(2,1)S(1)} %fusion.37), channel_id=1, source_target_pairs={{0,2},{1,3},{6,4},{7,5},{8,10},{9,11},{14,12},{15,13},{16,18},{17,... | collective-permute-start | bytes 1966088 | tf_op jit(solution)/shard_map/ppermute | solution.py:395
  74.0 20.9 %collective-permute-start.11 = (bf16[64,8192]{1,0:T(8,128)(2,1)}, bf16[64,8192]{1,0:T(8,128)(2,1)S(1)}, u32[]{:S(2)}, u32[]{:S(2)}) collective-permute-start(bf16[64,8192]{1,0:T(8,128)(2,1)} %collective-permute-done.9.refs_4_), channel_id=1, source_target_pairs={{2,4},{3,5},{4,6},{5,7},{10,12},{11,13},{12,14},{13,15},{18,20},{1... | collective-permute-start | bytes 3145736 | tf_op jit(solution)/shard_map/ppermute | solution.py:395
  76.1 25.9 %collective-permute-start.12 = (bf16[64,8192]{1,0:T(8,128)(2,1)S(1)}, bf16[64,8192]{1,0:T(8,128)(2,1)S(1)}, u32[]{:S(2)}, u32[]{:S(2)}) collective-permute-start(bf16[64,8192]{1,0:T(8,128)(2,1)S(1)} %collective-permute-done.7.refs_2_), channel_id=1, source_target_pairs={{2,0},{3,1},{4,2},{5,3},{10,8},{11,9},{12,10},{13,11},{18,16},{19,... | collective-permute-start | bytes 3145736 | tf_op jit(solution)/shard_map/ppermute | solution.py:395
  90.2 27.1 %collective-permute-start.4 = (bf16[160,2048]{1,0:T(8,128)(2,1)S(1)}, bf16[160,2048]{1,0:T(8,128)(2,1)S(1)}, u32[]{:S(2)}, u32[]{:S(2)}) collective-permute-start(bf16[160,2048]{1,0:T(8,128)(2,1)S(1)} %fusion.36), channel_id=1, source_target_pairs={{0,2},{1,3},{6,4},{7,5},{8,10},{9,11},{14,12},{15,13},{16,18},{17,... | collective-permute-start | bytes 1966088 | tf_op jit(solution)/shard_map/ppermute | solution.py:395
  94.9 24.1 %collective-permute-start.10 = (bf16[64,8192]{1,0:T(8,128)(2,1)}, bf16[64,8192]{1,0:T(8,128)(2,1)S(1)}, u32[]{:S(2)}, u32[]{:S(2)}) collective-permute-start(bf16[64,8192]{1,0:T(8,128)(2,1)} %collective-permute-done.9.refs_4_), channel_id=1, source_target_pairs={{0,1},{1,0},{2,3},{3,2},{4,5},{5,4},{6,7},{7,6},{8,9},{9,8},{10,11... | collective-permute-start | bytes 3145736 | tf_op jit(solution)/shard_map/ppermute | solution.py:389
  102.0 17.7 %collective-permute-start.8 = (bf16[64,8192]{1,0:T(8,128)(2,1)S(1)}, bf16[64,8192]{1,0:T(8,128)(2,1)S(1)}, u32[]{:S(2)}, u32[]{:S(2)}) collective-permute-start(bf16[64,8192]{1,0:T(8,128)(2,1)S(1)} %collective-permute-done.7.refs_2_), channel_id=1, source_target_pairs={{0,1},{1,0},{2,3},{3,2},{4,5},{5,4},{6,7},{7,6},{8,9},{9,8},{10,11... | collective-permute-start | bytes 3145736 | tf_op jit(solution)/shard_map/ppermute | solution.py:389
  104.2 16.2 %collective-permute-start.13 = (bf16[64,8192]{1,0:T(8,128)(2,1)S(1)}, bf16[64,8192]{1,0:T(8,128)(2,1)S(1)}, u32[]{:S(2)}, u32[]{:S(2)}) collective-permute-start(bf16[64,8192]{1,0:T(8,128)(2,1)S(1)} %broadcast_select_fusion.refs_6_), channel_id=1, source_target_pairs={{0,1},{1,0},{2,3},{3,2},{4,5},{5,4},{6,7},{7,6},{8,9},{9,8},{10,11... | collective-permute-start | bytes 3145736 | tf_op jit(solution)/shard_map/ppermute | solution.py:389
  120.4 47.2 %collective-permute-start.37 = (bf16[64,8192]{1,0:T(8,128)(2,1)S(1)}, bf16[64,8192]{1,0:T(8,128)(2,1)S(1)}, u32[]{:S(2)}, u32[]{:S(2)}) collective-permute-start(bf16[64,8192]{1,0:T(8,128)(2,1)S(1)} %broadcast_select_fusion.refs_6_), channel_id=1, source_target_pairs={{2,0},{3,1},{4,6},{5,7},{10,8},{11,9},{12,14},{13,15},{18,16},{19,... | collective-permute-start | bytes 3145736 | tf_op jit(solution)/shard_map/ppermute | solution.py:395
  128.3 53.4 %collective-permute-start.27 = (bf16[160,2048]{1,0:T(8,128)(2,1)S(1)}, bf16[160,2048]{1,0:T(8,128)(2,1)S(1)}, u32[]{:S(2)}, u32[]{:S(2)}) collective-permute-start(bf16[160,2048]{1,0:T(8,128)(2,1)S(1)} %fusion.34), channel_id=1, source_target_pairs={{2,0},{3,1},{4,6},{5,7},{10,8},{11,9},{12,14},{13,15},{18,16},{19,... | collective-permute-start | bytes 1966088 | tf_op jit(solution)/shard_map/ppermute | solution.py:395
  131.0 64.8 %collective-permute-start.23 = (bf16[160,2048]{1,0:T(8,128)(2,1)S(1)}, bf16[160,2048]{1,0:T(8,128)(2,1)S(1)}, u32[]{:S(2)}, u32[]{:S(2)}) collective-permute-start(bf16[160,2048]{1,0:T(8,128)(2,1)S(1)} %fusion.25), channel_id=1, source_target_pairs={{2,0},{3,1},{4,6},{5,7},{10,8},{11,9},{12,14},{13,15},{18,16},{19,... | collective-permute-start | bytes 1966088 | tf_op jit(solution)/shard_map/ppermute | solution.py:395
  133.4 76.4 %collective-permute-start.19 = (bf16[160,2048]{1,0:T(8,128)(2,1)S(1)}, bf16[160,2048]{1,0:T(8,128)(2,1)S(1)}, u32[]{:S(2)}, u32[]{:S(2)}) collective-permute-start(bf16[160,2048]{1,0:T(8,128)(2,1)S(1)} %fusion.16), channel_id=1, source_target_pairs={{2,0},{3,1},{4,6},{5,7},{10,8},{11,9},{12,14},{13,15},{18,16},{19,... | collective-permute-start | bytes 1966088 | tf_op jit(solution)/shard_map/ppermute | solution.py:395
  135.9 85.0 %collective-permute-start.14 = (bf16[160,2048]{1,0:T(8,128)(2,1)S(1)}, bf16[160,2048]{1,0:T(8,128)(2,1)S(1)}, u32[]{:S(2)}, u32[]{:S(2)}) collective-permute-start(bf16[160,2048]{1,0:T(8,128)(2,1)S(1)} %fusion.7), channel_id=1, source_target_pairs={{2,0},{3,1},{4,6},{5,7},{10,8},{11,9},{12,14},{13,15},{18,16},{19,... | collective-permute-start | bytes 1966088 | tf_op jit(solution)/shard_map/ppermute | solution.py:395
  167.7 53.3 %collective-permute-start.38 = (bf16[64,8192]{1,0:T(8,128)(2,1)S(1)}, bf16[64,8192]{1,0:T(8,128)(2,1)S(1)}, u32[]{:S(2)}, u32[]{:S(2)}) collective-permute-start(bf16[64,8192]{1,0:T(8,128)(2,1)S(1)} %collective-permute-done.37.refs_8_.refs_10_), channel_id=1, source_target_pairs={{0,1},{1,0},{2,3},{3,2},{4,5},{5,4},{6,7},{7,6},{8,9},{9,8},{10,11... | collective-permute-start | bytes 3145736 | tf_op jit(solution)/shard_map/ppermute | solution.py:389
  181.8 61.2 %collective-permute-start.30 = (bf16[160,2048]{1,0:T(8,128)(2,1)S(1)}, bf16[160,2048]{1,0:T(8,128)(2,1)S(1)}, u32[]{:S(2)}, u32[]{:S(2)}) collective-permute-start(bf16[160,2048]{1,0:T(8,128)(2,1)S(1)} %broadcast_select_fusion.1.refs_2_), channel_id=1, source_target_pairs={{0,1},{1,0},{2,3},{3,2},{4,5},{5,4},{6,7},{7,6},{8,9},{9,8},{10,11... | collective-permute-start | bytes 1966088 | tf_op jit(solution)/shard_map/ppermute | solution.py:389
  195.8 47.2 %collective-permute-start.29 = (bf16[160,2048]{1,0:T(8,128)(2,1)S(1)}, bf16[160,2048]{1,0:T(8,128)(2,1)S(1)}, u32[]{:S(2)}, u32[]{:S(2)}) collective-permute-start(bf16[160,2048]{1,0:T(8,128)(2,1)S(1)} %broadcast_select_fusion.2.refs_1_), channel_id=1, source_target_pairs={{0,1},{1,0},{2,3},{3,2},{4,5},{5,4},{6,7},{7,6},{8,9},{9,8},{10,11... | collective-permute-start | bytes 1966088 | tf_op jit(solution)/shard_map/ppermute | solution.py:389
  209.9 33.1 %collective-permute-start.28 = (bf16[160,2048]{1,0:T(8,128)(2,1)S(1)}, bf16[160,2048]{1,0:T(8,128)(2,1)S(1)}, u32[]{:S(2)}, u32[]{:S(2)}) collective-permute-start(bf16[160,2048]{1,0:T(8,128)(2,1)S(1)} %broadcast_select_fusion.3.refs_0_), channel_id=1, source_target_pairs={{0,1},{1,0},{2,3},{3,2},{4,5},{5,4},{6,7},{7,6},{8,9},{9,8},{10,11... | collective-permute-start | bytes 1966088 | tf_op jit(solution)/shard_map/ppermute | solution.py:389
  220.9 27.7 %collective-permute-start.15 = (bf16[160,2048]{1,0:T(8,128)(2,1)S(1)}, bf16[160,2048]{1,0:T(8,128)(2,1)S(1)}, u32[]{:S(2)}, u32[]{:S(2)}) collective-permute-start(bf16[160,2048]{1,0:T(8,128)(2,1)S(1)} %broadcast_select_fusion.4.l_ref.refs_3_), channel_id=1, source_target_pairs={{0,1},{1,0},{2,3},{3,2},{4,5},{5,4},{6,7},{7,6},{8,9},{9,8},{10,11... | collective-permute-start | bytes 1966088 | tf_op jit(solution)/shard_map/ppermute | solution.py:389
  (27 other events, 268.7 us)

commit v3 on v2

--- a/solution.py
+++ b/solution.py
@@ -124,6 +124,22 @@
 
 def stack(refs):
     return jnp.concatenate([r[...] for r in refs], axis=0)
+
+
+def early(table, seconds):
+    def kernel(table_ref, out_ref):
+        for k in range(table.shape[0]):
+            out_ref[k] = table_ref[k]
+
+    return pl.pallas_call(
+        kernel,
+        in_specs=[SMEM],
+        out_specs=SMEM,
+        out_shape=jax.ShapeDtypeStruct(table.shape, jnp.int32),
+        name="early",
+        compiler_params=vmem(1),
+        cost_estimate=cost(int(1e15 * seconds), 64),
+    )(table)
 
 
 def pick_rows(table, blocks, shifts):
@@ -436,6 +452,7 @@
 
     table = jnp.concatenate([jnp.stack([chip, core, me_x]).astype(jnp.int32), counts])
 
+    table = early(table, 25e-6)
     dy_packed, dy_ordered = pick_rows(table, dy_blocks, shifts)
     x_t = pick_columns(table, x_blocks)
     pre_packed = pick_wide(table, blocks, CHUNKS)

time: 269 us -> 262 us (0.974)
  local copies, waits for them, and re-layouts: 14.4 us -> 7.72 us
    unnamed x24 -> x30, local copies, waits for them, and re-layouts: 14.3 us -> 7.64 us
  transfers between devices with their start and end apart: 39 -> 39, of which waited for: 15 -> 15; matrix products, arithmetic and copies ran while one was open for 4% -> 4% of each run, Pallas kernels for 18% -> 19%
where the time goes in v3:
time: 262 us
  waiting for transfers between devices  136 us (52%)
  Pallas kernels  59.6 us (23%)
  starting transfers between devices  45.2 us (17%)
  other arithmetic  11.7 us (4%)
  local copies, waits for them, and re-layouts  7.72 us (3%)
    ppermute x17, waiting for transfers between devices, send(): return lax.ppermute(v, 'gy', chip_pairs(pairs))  126 us
    ppermute x17, starting transfers between devices, send(): return lax.ppermute(v, 'gy', chip_pairs(pairs))  32 us
    pallas_call x2, Pallas kernels, w_out_grad_of(): pl.pallas_call(kernel, grid_spec=pltpu.PrefetchScalarGridSpec(num_scalar_...  21.9 us
    ppermute x9, starting transfers between devices, swap_gx(): return lax.ppermute(v, 'gx', [(i, i ^ s) for i in range(shards)])  11.6 us
    pallas_call x1, Pallas kernels, w_in_grad_of(): pl.pallas_call(kernel, grid=(chunks,), in_specs=[pl.BlockSpec((model, liv...  11.5 us
    ppermute x9, waiting for transfers between devices, swap_gx(): return lax.ppermute(v, 'gx', [(i, i ^ s) for i in range(shards)])  10.3 us
    pallas_call x3, Pallas kernels, hidden_sums(): pl.pallas_call(kernel, grid=(chunks * split,), in_specs=[pl.BlockSpec((li...  8.03 us
    unnamed x30, local copies, waits for them, and re-layouts  7.64 us
  transfers between devices with their start and end apart: 39, of which 15 were waited for; matrix products, arithmetic and copies ran while one was open for 4% of the time, Pallas kernels for 19%

profile of v3, /device:TPU:0, one launch (start us, length us, event | category | flops | bytes accessed | tf_op | source)
XLA Modules:
  0.0 261.6 jit_solution(8558023538167890753)
XLA Ops:
  0.6 3.0 %collective-permute-start = (bf16[128,1024]{1,0:T(8,128)(2,1)}, bf16[128,1024]{1,0:T(8,128)(2,1)S(1)}, u32[]{:S(2)}, u32[]{:S(2)}) collective-permute-start(bf16[128,1024]{1,0:T(8,128)(2,1)} %refs_0_.5), channel_id=1, source_target_pairs={{0,8},{8,0},{16,24},{24,16},{1,9},{9,1},{17,25},{25,17},{2,10},{10... | collective-permute-start | bytes 786440 | tf_op jit(solution)/shard_map/ppermute | solution.py:408
  7.3 3.8 %collective-permute-done.refs_1_ = bf16[128,1024]{1,0:T(8,128)(2,1)S(1)} collective-permute-done((bf16[128,1024]{1,0:T(8,128)(2,1)}, bf16[128,1024]{1,0:T(8,128)(2,1)S(1)}, u32[]{:S(2)}, u32[]{:S(2)}) %collective-permute-start) | collective-permute-done | bytes 262176 | tf_op jit(solution)/shard_map/ppermute | solution.py:408
  11.0 6.2 %collective-permute-done.1.refs_2_ = bf16[128,1024]{1,0:T(8,128)(2,1)S(1)} collective-permute-done((bf16[128,1024]{1,0:T(8,128)(2,1)}, bf16[128,1024]{1,0:T(8,128)(2,1)S(1)}, u32[]{:S(2)}, u32[]{:S(2)}) %collective-permute-start.1) | collective-permute-done | bytes 262176 | tf_op jit(solution)/shard_map/ppermute | solution.py:408
  19.9 4.3 %hidden_sums.3 = (f32[160,2048]{1,0:T(8,128)S(1)}, bf16[160,2048]{1,0:T(8,128)(2,1)}, f32[160,2048]{1,0:T(8,128)S(1)}, bf16[160,2048]{1,0:T(8,128)(2,1)S(1)}) custom-call(bf16[320,1024]{1,0:T(8,128)(2,1)S(1)} %get-tuple-element.21.dy_ref, bf16[8192,1024]{1,0:T(8,128)(2,1)S(1)} %bitcast.6), custom_call_target="tpu_custom_call" | custom-call | flops 2684354560 | bytes 8388608 | tf_op jit(solution)/shard_map/hidden_sums/pallas_call | solution.py:236
  28.5 4.5 %collective-permute-start.9 = (bf16[64,8192]{1,0:T(8,128)(2,1)}, bf16[64,8192]{1,0:T(8,128)(2,1)}, u32[]{:S(2)}, u32[]{:S(2)}) collective-permute-start(bf16[64,8192]{1,0:T(8,128)(2,1)} %refs_0_.9), channel_id=1, source_target_pairs={{0,2},{1,3},{2,4},{3,5},{4,6},{5,7},{8,10},{9,11},{10,12},{11,13},... | collective-permute-start | bytes 3145736 | tf_op jit(solution)/shard_map/ppermute | solution.py:411
  33.1 5.8 %copy-done = bf16[8192,1024]{1,0:T(8,128)(2,1)S(1)} copy-done((bf16[8192,1024]{1,0:T(8,128)(2,1)S(1)}, bf16[8192,1024]{1,0:T(8,128)(2,1)}, u32[]{:S(2)}) %copy-start) | copy-done | bytes 16777240
  48.7 4.6 %collective-permute-start.25 = (bf16[160,2048]{1,0:T(8,128)(2,1)S(1)}, bf16[160,2048]{1,0:T(8,128)(2,1)S(1)}, u32[]{:S(2)}, u32[]{:S(2)}) collective-permute-start(bf16[160,2048]{1,0:T(8,128)(2,1)S(1)} %fusion.39), channel_id=1, source_target_pairs={{0,2},{1,3},{6,4},{7,5},{8,10},{9,11},{14,12},{15,13},{16,18},{17,... | collective-permute-start | bytes 1966088 | tf_op jit(solution)/shard_map/ppermute | solution.py:411
  55.5 4.4 %collective-permute-start.17 = (bf16[160,2048]{1,0:T(8,128)(2,1)S(1)}, bf16[160,2048]{1,0:T(8,128)(2,1)S(1)}, u32[]{:S(2)}, u32[]{:S(2)}) collective-permute-start(bf16[160,2048]{1,0:T(8,128)(2,1)S(1)} %fusion.37), channel_id=1, source_target_pairs={{0,2},{1,3},{6,4},{7,5},{8,10},{9,11},{14,12},{15,13},{16,18},{17,... | collective-permute-start | bytes 1966088 | tf_op jit(solution)/shard_map/ppermute | solution.py:411
  60.0 7.4 %collective-permute-done.7.refs_2_ = bf16[64,8192]{1,0:T(8,128)(2,1)S(1)} collective-permute-done((bf16[64,8192]{1,0:T(8,128)(2,1)}, bf16[64,8192]{1,0:T(8,128)(2,1)S(1)}, u32[]{:S(2)}, u32[]{:S(2)}) %collective-permute-start.7) | collective-permute-done | bytes 1048608 | tf_op jit(solution)/shard_map/ppermute | solution.py:411
  72.1 11.4 %collective-permute-done.21 = bf16[160,2048]{1,0:T(8,128)(2,1)S(1)} collective-permute-done((bf16[160,2048]{1,0:T(8,128)(2,1)S(1)}, bf16[160,2048]{1,0:T(8,128)(2,1)S(1)}, u32[]{:S(2)}, u32[]{:S(2)}) %collective-permute-start.21) | collective-permute-done | bytes 655392 | tf_op jit(solution)/shard_map/ppermute | solution.py:411
  83.5 4.4 %collective-permute-start.4 = (bf16[160,2048]{1,0:T(8,128)(2,1)S(1)}, bf16[160,2048]{1,0:T(8,128)(2,1)S(1)}, u32[]{:S(2)}, u32[]{:S(2)}) collective-permute-start(bf16[160,2048]{1,0:T(8,128)(2,1)S(1)} %fusion.36), channel_id=1, source_target_pairs={{0,2},{1,3},{6,4},{7,5},{8,10},{9,11},{14,12},{15,13},{16,18},{17,... | collective-permute-start | bytes 1966088 | tf_op jit(solution)/shard_map/ppermute | solution.py:411
  88.3 7.0 %collective-permute-done.12 = bf16[64,8192]{1,0:T(8,128)(2,1)S(1)} collective-permute-done((bf16[64,8192]{1,0:T(8,128)(2,1)S(1)}, bf16[64,8192]{1,0:T(8,128)(2,1)S(1)}, u32[]{:S(2)}, u32[]{:S(2)}) %collective-permute-start.12) | collective-permute-done | bytes 1048608 | tf_op jit(solution)/shard_map/ppermute | solution.py:411
  97.8 12.8 %collective-permute-done.4 = bf16[160,2048]{1,0:T(8,128)(2,1)S(1)} collective-permute-done((bf16[160,2048]{1,0:T(8,128)(2,1)S(1)}, bf16[160,2048]{1,0:T(8,128)(2,1)S(1)}, u32[]{:S(2)}, u32[]{:S(2)}) %collective-permute-start.4) | collective-permute-done | bytes 655392 | tf_op jit(solution)/shard_map/ppermute | solution.py:411
  115.1 4.3 %pick_wide.1 = (bf16[160,2048]{1,0:T(8,128)(2,1)S(1)}, bf16[160,2048]{1,0:T(8,128)(2,1)S(1)}, bf16[160,2048]{1,0:T(8,128)(2,1)S(1)}, bf16[160,2048]{1,0:T(8,128)(2,1)S(1)}) custom-call(s32[7]{0:T(128)S(1)} %early.1.table_ref, bf16[64,8192]{1,0:T(8,128)(2,1)} %refs_0_.9, bf16[64,8192]{1,0:T(8,128)(2,1)S(1)} %collective-permute-done.6.refs_1_, ...), custom_call_target="tpu_custom_call" | custom-call | flops 1342177280 | bytes 11010048 | tf_op jit(solution)/shard_map/pick_wide/pallas_call | solution.py:204
  130.5 30.5 %collective-permute-done.37.refs_8_.refs_10_ = bf16[64,8192]{1,0:T(8,128)(2,1)S(1)} collective-permute-done((bf16[64,8192]{1,0:T(8,128)(2,1)S(1)}, bf16[64,8192]{1,0:T(8,128)(2,1)S(1)}, u32[]{:S(2)}, u32[]{:S(2)}) %collective-permute-start.37) | collective-permute-done | bytes 1048608 | tf_op jit(solution)/shard_map/ppermute | solution.py:411
  161.0 14.0 %collective-permute-done.27 = bf16[160,2048]{1,0:T(8,128)(2,1)S(1)} collective-permute-done((bf16[160,2048]{1,0:T(8,128)(2,1)S(1)}, bf16[160,2048]{1,0:T(8,128)(2,1)S(1)}, u32[]{:S(2)}, u32[]{:S(2)}) %collective-permute-start.27) | collective-permute-done | bytes 655392 | tf_op jit(solution)/shard_map/ppermute | solution.py:411
  175.2 13.9 %collective-permute-done.23 = bf16[160,2048]{1,0:T(8,128)(2,1)S(1)} collective-permute-done((bf16[160,2048]{1,0:T(8,128)(2,1)S(1)}, bf16[160,2048]{1,0:T(8,128)(2,1)S(1)}, u32[]{:S(2)}, u32[]{:S(2)}) %collective-permute-start.23) | collective-permute-done | bytes 655392 | tf_op jit(solution)/shard_map/ppermute | solution.py:411
  189.2 13.9 %collective-permute-done.19 = bf16[160,2048]{1,0:T(8,128)(2,1)S(1)} collective-permute-done((bf16[160,2048]{1,0:T(8,128)(2,1)S(1)}, bf16[160,2048]{1,0:T(8,128)(2,1)S(1)}, u32[]{:S(2)}, u32[]{:S(2)}) %collective-permute-start.19) | collective-permute-done | bytes 655392 | tf_op jit(solution)/shard_map/ppermute | solution.py:411
  203.3 10.9 %collective-permute-done.14 = bf16[160,2048]{1,0:T(8,128)(2,1)S(1)} collective-permute-done((bf16[160,2048]{1,0:T(8,128)(2,1)S(1)}, bf16[160,2048]{1,0:T(8,128)(2,1)S(1)}, u32[]{:S(2)}, u32[]{:S(2)}) %collective-permute-start.14) | collective-permute-done | bytes 655392 | tf_op jit(solution)/shard_map/ppermute | solution.py:411
  214.4 11.0 %w_out_grad_of.2.refs_12_ = bf16[8192,1024]{1,0:T(8,128)(2,1)} custom-call(s32[8]{0:T(128)S(1)} %stack.33.flag_ref, bf16[512,1024]{1,0:T(8,128)(2,1)S(1)} %copy-done.2, bf16[64,8192]{1,0:T(8,128)(2,1)} %refs_0_.9, bf16[64,8192]{1,0:T(8,128)(2,1)S(1)} %collective-permute-done.6.refs_1_, bf16[64,8192]{1,0:T(8,128)(2,1)S(1)} %collective-permute-done.7.refs_2_, ...), custom_call_target="tpu_custom_call" | custom-call | flops 4294967296 | bytes 12582912 | tf_op jit(solution)/shard_map/w_out_grad_of/pallas_call | solution.py:370
  225.4 11.0 %w_out_grad_of.3 = bf16[8192,1024]{1,0:T(8,128)(2,1)} custom-call(s32[8]{0:T(128)S(1)} %stack.33.flag_ref, bf16[512,1024]{1,0:T(8,128)(2,1)S(1)} %copy-done.2, bf16[64,8192]{1,0:T(8,128)(2,1)} %refs_0_.9, bf16[64,8192]{1,0:T(8,128)(2,1)S(1)} %collective-permute-done.6.refs_1_, ...), custom_call_target="tpu_custom_call", output_to_operand_aliasing={{}: (14, {})} | custom-call | flops 4294967296 | bytes 12582912 | tf_op jit(solution)/shard_map/w_out_grad_of/pallas_call | solution.py:370
  236.4 5.6 %in_sum_of.1.before_ref = f32[320,1024]{1,0:T(8,128)S(1)} custom-call(bf16[160,2048]{1,0:T(8,128)(2,1)S(1)} %broadcast_select_fusion.3.refs_0_, bf16[160,2048]{1,0:T(8,128)(2,1)S(1)} %broadcast_select_fusion.2.refs_1_, bf16[160,2048]{1,0:T(8,128)(2,1)S(1)} %broadcast_select_fusion.1.refs_2_, bf16[160,2048]{1,0:T(8,128)(2,1)S(1)} %collective-permute-done.28.refs_3_.refs_4_, ...), custom_call_target="tpu_custom_call" | custom-call | flops 4026531840 | bytes 12582912 | tf_op jit(solution)/shard_map/in_sum_of/pallas_call | solution.py:267
  242.0 3.5 %in_last.1 = (bf16[128,1024]{1,0:T(8,128)(2,1)S(1)}, bf16[128,1024]{1,0:T(8,128)(2,1)S(1)}, bf16[128,1024]{1,0:T(8,128)(2,1)S(1)}, bf16[128,1024]{1,0:T(8,128)(2,1)S(1)}) custom-call(s32[7]{0:T(128)S(1)} %early.1.table_ref, bf16[160,2048]{1,0:T(8,128)(2,1)S(1)} %broadcast_select_fusion.4.l_ref.refs_3_, ...), custom_call_target="tpu_custom_call" | custom-call | flops 1342177280 | bytes 6160384 | tf_op jit(solution)/shard_map/in_last/pallas_call | solution.py:300
  249.0 11.5 %w_in_grad_of.1 = bf16[1024,8192]{1,0:T(8,128)(2,1)} custom-call(bf16[1024,320]{1,0:T(8,128)(2,1)S(1)} %pick_columns.1.x_ref, bf16[160,2048]{1,0:T(8,128)(2,1)S(1)} %broadcast_select_fusion.3.refs_0_, bf16[160,2048]{1,0:T(8,128)(2,1)S(1)} %broadcast_select_fusion.2.refs_1_, bf16[160,2048]{1,0:T(8,128)(2,1)S(1)} %broadcast_select_fusion.1.refs_2_, ...), custom_call_target="tpu_custom_call" | custom-call | flops 5368709120 | bytes 16777216 | tf_op jit(solution)/shard_map/w_in_grad_of/pallas_call | solution.py:333
  (119 shorter events, 50.9 us)
Async XLA Ops:
  25.0 21.5 %collective-permute-start.24 = (bf16[160,2048]{1,0:T(8,128)(2,1)}, bf16[160,2048]{1,0:T(8,128)(2,1)}, u32[]{:S(2)}, u32[]{:S(2)}) collective-permute-start(bf16[160,2048]{1,0:T(8,128)(2,1)} %get-tuple-element.32), channel_id=1, source_target_pairs={{0,1},{1,0},{2,3},{3,2},{4,5},{5,4},{6,7},{7,6},{8,9},{9,8},{10,11... | collective-permute-start | bytes 1966088 | tf_op jit(solution)/shard_map/ppermute | solution.py:405
  26.3 15.8 %collective-permute-start.35 = (bf16[128,1024]{1,0:T(8,128)(2,1)S(1)}, bf16[128,1024]{1,0:T(8,128)(2,1)}, u32[]{:S(2)}, u32[]{:S(2)}) collective-permute-start(bf16[128,1024]{1,0:T(8,128)(2,1)S(1)} %copy-done.3), channel_id=1, source_target_pairs={{0,16},{8,24},{16,0},{24,8},{1,17},{9,25},{17,1},{25,9},{2,18},{10... | collective-permute-start | bytes 786440 | tf_op jit(solution)/shard_map/ppermute | solution.py:408
  28.5 27.0 %collective-permute-start.9 = (bf16[64,8192]{1,0:T(8,128)(2,1)}, bf16[64,8192]{1,0:T(8,128)(2,1)}, u32[]{:S(2)}, u32[]{:S(2)}) collective-permute-start(bf16[64,8192]{1,0:T(8,128)(2,1)} %refs_0_.9), channel_id=1, source_target_pairs={{0,2},{1,3},{2,4},{3,5},{4,6},{5,7},{8,10},{9,11},{10,12},{11,13},... | collective-permute-start | bytes 3145736 | tf_op jit(solution)/shard_map/ppermute | solution.py:411
  40.8 26.6 %collective-permute-start.7 = (bf16[64,8192]{1,0:T(8,128)(2,1)}, bf16[64,8192]{1,0:T(8,128)(2,1)S(1)}, u32[]{:S(2)}, u32[]{:S(2)}) collective-permute-start(bf16[64,8192]{1,0:T(8,128)(2,1)} %refs_0_.9), channel_id=1, source_target_pairs={{2,0},{3,1},{4,2},{5,3},{6,4},{7,5},{10,8},{11,9},{12,10},{13,11},... | collective-permute-start | bytes 3145736 | tf_op jit(solution)/shard_map/ppermute | solution.py:411
  42.1 69.5 %collective-permute-start.6 = (bf16[64,8192]{1,0:T(8,128)(2,1)}, bf16[64,8192]{1,0:T(8,128)(2,1)S(1)}, u32[]{:S(2)}, u32[]{:S(2)}) collective-permute-start(bf16[64,8192]{1,0:T(8,128)(2,1)} %refs_0_.9), channel_id=1, source_target_pairs={{0,1},{1,0},{2,3},{3,2},{4,5},{5,4},{6,7},{7,6},{8,9},{9,8},{10,11... | collective-permute-start | bytes 3145736 | tf_op jit(solution)/shard_map/ppermute | solution.py:405
  48.7 20.8 %collective-permute-start.25 = (bf16[160,2048]{1,0:T(8,128)(2,1)S(1)}, bf16[160,2048]{1,0:T(8,128)(2,1)S(1)}, u32[]{:S(2)}, u32[]{:S(2)}) collective-permute-start(bf16[160,2048]{1,0:T(8,128)(2,1)S(1)} %fusion.39), channel_id=1, source_target_pairs={{0,2},{1,3},{6,4},{7,5},{8,10},{9,11},{14,12},{15,13},{16,18},{17,... | collective-permute-start | bytes 1966088 | tf_op jit(solution)/shard_map/ppermute | solution.py:411
  53.5 30.1 %collective-permute-start.21 = (bf16[160,2048]{1,0:T(8,128)(2,1)S(1)}, bf16[160,2048]{1,0:T(8,128)(2,1)S(1)}, u32[]{:S(2)}, u32[]{:S(2)}) collective-permute-start(bf16[160,2048]{1,0:T(8,128)(2,1)S(1)} %fusion.38), channel_id=1, source_target_pairs={{0,2},{1,3},{6,4},{7,5},{8,10},{9,11},{14,12},{15,13},{16,18},{17,... | collective-permute-start | bytes 1966088 | tf_op jit(solution)/shard_map/ppermute | solution.py:411
  55.5 42.0 %collective-permute-start.17 = (bf16[160,2048]{1,0:T(8,128)(2,1)S(1)}, bf16[160,2048]{1,0:T(8,128)(2,1)S(1)}, u32[]{:S(2)}, u32[]{:S(2)}) collective-permute-start(bf16[160,2048]{1,0:T(8,128)(2,1)S(1)} %fusion.37), channel_id=1, source_target_pairs={{0,2},{1,3},{6,4},{7,5},{8,10},{9,11},{14,12},{15,13},{16,18},{17,... | collective-permute-start | bytes 1966088 | tf_op jit(solution)/shard_map/ppermute | solution.py:411
  67.4 20.9 %collective-permute-start.11 = (bf16[64,8192]{1,0:T(8,128)(2,1)}, bf16[64,8192]{1,0:T(8,128)(2,1)S(1)}, u32[]{:S(2)}, u32[]{:S(2)}) collective-permute-start(bf16[64,8192]{1,0:T(8,128)(2,1)} %collective-permute-done.9.refs_4_), channel_id=1, source_target_pairs={{2,4},{3,5},{4,6},{5,7},{10,12},{11,13},{12,14},{13,15},{18,20},{1... | collective-permute-start | bytes 3145736 | tf_op jit(solution)/shard_map/ppermute | solution.py:411
  69.5 25.9 %collective-permute-start.12 = (bf16[64,8192]{1,0:T(8,128)(2,1)S(1)}, bf16[64,8192]{1,0:T(8,128)(2,1)S(1)}, u32[]{:S(2)}, u32[]{:S(2)}) collective-permute-start(bf16[64,8192]{1,0:T(8,128)(2,1)S(1)} %collective-permute-done.7.refs_2_), channel_id=1, source_target_pairs={{2,0},{3,1},{4,2},{5,3},{10,8},{11,9},{12,10},{13,11},{18,16},{19,... | collective-permute-start | bytes 3145736 | tf_op jit(solution)/shard_map/ppermute | solution.py:411
  83.5 27.1 %collective-permute-start.4 = (bf16[160,2048]{1,0:T(8,128)(2,1)S(1)}, bf16[160,2048]{1,0:T(8,128)(2,1)S(1)}, u32[]{:S(2)}, u32[]{:S(2)}) collective-permute-start(bf16[160,2048]{1,0:T(8,128)(2,1)S(1)} %fusion.36), channel_id=1, source_target_pairs={{0,2},{1,3},{6,4},{7,5},{8,10},{9,11},{14,12},{15,13},{16,18},{17,... | collective-permute-start | bytes 1966088 | tf_op jit(solution)/shard_map/ppermute | solution.py:411
  88.2 24.1 %collective-permute-start.10 = (bf16[64,8192]{1,0:T(8,128)(2,1)}, bf16[64,8192]{1,0:T(8,128)(2,1)S(1)}, u32[]{:S(2)}, u32[]{:S(2)}) collective-permute-start(bf16[64,8192]{1,0:T(8,128)(2,1)} %collective-permute-done.9.refs_4_), channel_id=1, source_target_pairs={{0,1},{1,0},{2,3},{3,2},{4,5},{5,4},{6,7},{7,6},{8,9},{9,8},{10,11... | collective-permute-start | bytes 3145736 | tf_op jit(solution)/shard_map/ppermute | solution.py:405
  95.3 17.7 %collective-permute-start.8 = (bf16[64,8192]{1,0:T(8,128)(2,1)S(1)}, bf16[64,8192]{1,0:T(8,128)(2,1)S(1)}, u32[]{:S(2)}, u32[]{:S(2)}) collective-permute-start(bf16[64,8192]{1,0:T(8,128)(2,1)S(1)} %collective-permute-done.7.refs_2_), channel_id=1, source_target_pairs={{0,1},{1,0},{2,3},{3,2},{4,5},{5,4},{6,7},{7,6},{8,9},{9,8},{10,11... | collective-permute-start | bytes 3145736 | tf_op jit(solution)/shard_map/ppermute | solution.py:405
  97.6 16.2 %collective-permute-start.13 = (bf16[64,8192]{1,0:T(8,128)(2,1)S(1)}, bf16[64,8192]{1,0:T(8,128)(2,1)S(1)}, u32[]{:S(2)}, u32[]{:S(2)}) collective-permute-start(bf16[64,8192]{1,0:T(8,128)(2,1)S(1)} %broadcast_select_fusion.refs_6_), channel_id=1, source_target_pairs={{0,1},{1,0},{2,3},{3,2},{4,5},{5,4},{6,7},{7,6},{8,9},{9,8},{10,11... | collective-permute-start | bytes 3145736 | tf_op jit(solution)/shard_map/ppermute | solution.py:405
  113.8 47.2 %collective-permute-start.37 = (bf16[64,8192]{1,0:T(8,128)(2,1)S(1)}, bf16[64,8192]{1,0:T(8,128)(2,1)S(1)}, u32[]{:S(2)}, u32[]{:S(2)}) collective-permute-start(bf16[64,8192]{1,0:T(8,128)(2,1)S(1)} %broadcast_select_fusion.refs_6_), channel_id=1, source_target_pairs={{2,0},{3,1},{4,6},{5,7},{10,8},{11,9},{12,14},{13,15},{18,16},{19,... | collective-permute-start | bytes 3145736 | tf_op jit(solution)/shard_map/ppermute | solution.py:411
  121.7 53.3 %collective-permute-start.27 = (bf16[160,2048]{1,0:T(8,128)(2,1)S(1)}, bf16[160,2048]{1,0:T(8,128)(2,1)S(1)}, u32[]{:S(2)}, u32[]{:S(2)}) collective-permute-start(bf16[160,2048]{1,0:T(8,128)(2,1)S(1)} %fusion.34), channel_id=1, source_target_pairs={{2,0},{3,1},{4,6},{5,7},{10,8},{11,9},{12,14},{13,15},{18,16},{19,... | collective-permute-start | bytes 1966088 | tf_op jit(solution)/shard_map/ppermute | solution.py:411
  124.3 64.8 %collective-permute-start.23 = (bf16[160,2048]{1,0:T(8,128)(2,1)S(1)}, bf16[160,2048]{1,0:T(8,128)(2,1)S(1)}, u32[]{:S(2)}, u32[]{:S(2)}) collective-permute-start(bf16[160,2048]{1,0:T(8,128)(2,1)S(1)} %fusion.25), channel_id=1, source_target_pairs={{2,0},{3,1},{4,6},{5,7},{10,8},{11,9},{12,14},{13,15},{18,16},{19,... | collective-permute-start | bytes 1966088 | tf_op jit(solution)/shard_map/ppermute | solution.py:411
  126.8 76.3 %collective-permute-start.19 = (bf16[160,2048]{1,0:T(8,128)(2,1)S(1)}, bf16[160,2048]{1,0:T(8,128)(2,1)S(1)}, u32[]{:S(2)}, u32[]{:S(2)}) collective-permute-start(bf16[160,2048]{1,0:T(8,128)(2,1)S(1)} %fusion.16), channel_id=1, source_target_pairs={{2,0},{3,1},{4,6},{5,7},{10,8},{11,9},{12,14},{13,15},{18,16},{19,... | collective-permute-start | bytes 1966088 | tf_op jit(solution)/shard_map/ppermute | solution.py:411
  129.2 84.9 %collective-permute-start.14 = (bf16[160,2048]{1,0:T(8,128)(2,1)S(1)}, bf16[160,2048]{1,0:T(8,128)(2,1)S(1)}, u32[]{:S(2)}, u32[]{:S(2)}) collective-permute-start(bf16[160,2048]{1,0:T(8,128)(2,1)S(1)} %fusion.7), channel_id=1, source_target_pairs={{2,0},{3,1},{4,6},{5,7},{10,8},{11,9},{12,14},{13,15},{18,16},{19,... | collective-permute-start | bytes 1966088 | tf_op jit(solution)/shard_map/ppermute | solution.py:411
  161.0 53.3 %collective-permute-start.38 = (bf16[64,8192]{1,0:T(8,128)(2,1)S(1)}, bf16[64,8192]{1,0:T(8,128)(2,1)S(1)}, u32[]{:S(2)}, u32[]{:S(2)}) collective-permute-start(bf16[64,8192]{1,0:T(8,128)(2,1)S(1)} %collective-permute-done.37.refs_8_.refs_10_), channel_id=1, source_target_pairs={{0,1},{1,0},{2,3},{3,2},{4,5},{5,4},{6,7},{7,6},{8,9},{9,8},{10,11... | collective-permute-start | bytes 3145736 | tf_op jit(solution)/shard_map/ppermute | solution.py:405
  175.1 61.2 %collective-permute-start.30 = (bf16[160,2048]{1,0:T(8,128)(2,1)S(1)}, bf16[160,2048]{1,0:T(8,128)(2,1)S(1)}, u32[]{:S(2)}, u32[]{:S(2)}) collective-permute-start(bf16[160,2048]{1,0:T(8,128)(2,1)S(1)} %broadcast_select_fusion.1.refs_2_), channel_id=1, source_target_pairs={{0,1},{1,0},{2,3},{3,2},{4,5},{5,4},{6,7},{7,6},{8,9},{9,8},{10,11... | collective-permute-start | bytes 1966088 | tf_op jit(solution)/shard_map/ppermute | solution.py:405
  189.2 47.2 %collective-permute-start.29 = (bf16[160,2048]{1,0:T(8,128)(2,1)S(1)}, bf16[160,2048]{1,0:T(8,128)(2,1)S(1)}, u32[]{:S(2)}, u32[]{:S(2)}) collective-permute-start(bf16[160,2048]{1,0:T(8,128)(2,1)S(1)} %broadcast_select_fusion.2.refs_1_), channel_id=1, source_target_pairs={{0,1},{1,0},{2,3},{3,2},{4,5},{5,4},{6,7},{7,6},{8,9},{9,8},{10,11... | collective-permute-start | bytes 1966088 | tf_op jit(solution)/shard_map/ppermute | solution.py:405
  203.2 33.1 %collective-permute-start.28 = (bf16[160,2048]{1,0:T(8,128)(2,1)S(1)}, bf16[160,2048]{1,0:T(8,128)(2,1)S(1)}, u32[]{:S(2)}, u32[]{:S(2)}) collective-permute-start(bf16[160,2048]{1,0:T(8,128)(2,1)S(1)} %broadcast_select_fusion.3.refs_0_), channel_id=1, source_target_pairs={{0,1},{1,0},{2,3},{3,2},{4,5},{5,4},{6,7},{7,6},{8,9},{9,8},{10,11... | collective-permute-start | bytes 1966088 | tf_op jit(solution)/shard_map/ppermute | solution.py:405
  214.2 27.7 %collective-permute-start.15 = (bf16[160,2048]{1,0:T(8,128)(2,1)S(1)}, bf16[160,2048]{1,0:T(8,128)(2,1)S(1)}, u32[]{:S(2)}, u32[]{:S(2)}) collective-permute-start(bf16[160,2048]{1,0:T(8,128)(2,1)S(1)} %broadcast_select_fusion.4.l_ref.refs_3_), channel_id=1, source_target_pairs={{0,1},{1,0},{2,3},{3,2},{4,5},{5,4},{6,7},{7,6},{8,9},{9,8},{10,11... | collective-permute-start | bytes 1966088 | tf_op jit(solution)/shard_map/ppermute | solution.py:405
  (30 other events, 329.4 us)
